TPU v7x, 512 devices: a whole 4x8x8 slice. The times are simulated.
512 devices in a mesh: dom: 16 (over z_hi, y), rel: 32 (over z_lo, x, core).
Axes of the slice: x: 4, y: 8, z: 8 (z_hi: 2, z_lo: 4; z = z_hi * 4 + z_lo), core: 2. Of those that a mesh axis runs over, the one named last changes fastest.
Arguments:
- entity: float32 [65536, 512], P(('dom', 'rel')), may hold values from -1.8 to 1.8
- entity_acc: float32 [65536, 512], P(('dom', 'rel')), may hold values from 0.01 to 1
- relation: float32 [4096, 512], P('rel'), may hold values from -1 to 1, as said below
- relation_acc: float32 [4096, 512], P('rel'), may hold values from 0.01 to 1
- send_rows: int32 [512, 32, 16], P(('dom', 'rel')), may hold values from 0 to 127, as said below
- trip_head: int32 [131072], P(('dom', 'rel')), may hold values from 0 to 511
- trip_rel: int32 [131072], P(('dom', 'rel')), may hold values from 0 to 127
- trip_tail: int32 [131072], P(('dom', 'rel')), may hold values from 0 to 511
- neg_part: int32 [1], replicated, may hold values from 0 to 15
- neg_rows: int32 [32, 32], replicated, may hold values from 0 to 127
Outputs:
- new_entity: float32 [65536, 512], P(('dom', 'rel'))
- new_entity_acc: float32 [65536, 512], P(('dom', 'rel'))
- new_relation: float32 [4096, 512], P('rel')
- new_relation_acc: float32 [4096, 512], P('rel')
Inputs may be any that keep to these rules, and one draw needn't show every extreme that they name: `send_rows`: within one owner's list for one receiver the 16 rows are distinct. `relation`: every component has magnitude 0.1 or more.
All inputs are finite; a program needn't handle non-finite values.
Results may differ from a plain program's by a relative error of at most 0.0003.
Values sent between devices are 32-bit elements; how exact they have to be, the bound alone decides.
A program may use at most 64 MiB of HBM per device.

v0:
```python
import jax
import jax.numpy as jnp
from jax import lax
from jax.sharding import PartitionSpec as P

step_size = 0.05


def broadcast(block, axis, owner):
    block = jnp.where(lax.axis_index(axis) == owner, block, jnp.zeros_like(block))
    return lax.psum(block, axis)


def hamilton(left, right):
    left_a, left_b, left_c, left_d = jnp.split(left, 4, axis=-1)
    right_a, right_b, right_c, right_d = jnp.split(right, 4, axis=-1)
    out_a = left_a * right_a - left_b * right_b - left_c * right_c - left_d * right_d
    out_b = left_a * right_b + left_b * right_a + left_c * right_d - left_d * right_c
    out_c = left_a * right_c - left_b * right_d + left_c * right_a + left_d * right_b
    out_d = left_a * right_d + left_b * right_c - left_c * right_b + left_d * right_a
    return jnp.concatenate([out_a, out_b, out_c, out_d], axis=-1)


def unit_rel(relation):
    comp_a, comp_b, comp_c, comp_d = jnp.split(relation, 4, axis=-1)
    magnitude = jnp.sqrt(comp_a * comp_a + comp_b * comp_b + comp_c * comp_c + comp_d * comp_d)
    return relation / jnp.concatenate([magnitude, magnitude, magnitude, magnitude], axis=-1)


def local_loss(touched, relation, negatives, heads, rels, tails):
    unit_rows = unit_rel(relation)
    one_hot = (rels[:, None] == jnp.arange(relation.shape[0])[None, :]).astype(unit_rows.dtype)
    rotation = jnp.dot(one_hot, unit_rows, precision=lax.Precision.HIGHEST)
    query = hamilton(touched[heads], rotation)
    positive = jnp.sum(query * touched[tails], axis=-1)
    scores = jnp.einsum("ik,jk->ij", query, negatives, precision=lax.Precision.HIGHEST)
    return (
        jnp.sum(jax.nn.softplus(-positive)) + jnp.sum(jax.nn.softplus(scores)) / negatives.shape[0]
    )


def adagrad(values, history, gradient):
    history_new = history + gradient * gradient
    return (values - step_size * gradient / jnp.sqrt(history_new), history_new)


def shards(
    entity,
    entity_acc,
    relation,
    relation_acc,
    send_rows,
    trip_head,
    trip_rel,
    trip_tail,
    neg_part,
    neg_rows,
):
    row_width = entity.shape[1]
    send_lists = send_rows[0]
    outgoing = entity[send_lists]
    touched = lax.all_to_all(outgoing, "rel", split_axis=0, concat_axis=0, tiled=True).reshape(
        -1, row_width
    )
    neg_root = neg_part[0]
    rel_here = lax.axis_index("rel")
    own_negs = entity[neg_rows[rel_here]]
    grouped = lax.all_gather(own_negs, "rel", axis=0, tiled=True)
    negatives = broadcast(grouped, "dom", neg_root)

    def scored(touched_in, relation_in, negatives_in):
        return local_loss(touched_in, relation_in, negatives_in, trip_head, trip_rel, trip_tail)

    loss_value, pullback = jax.vjp(scored, touched, relation, negatives)
    grad_rows, grad_rel, grad_neg = pullback(jnp.ones_like(loss_value))
    returned = lax.all_to_all(
        grad_rows.reshape(-1, send_lists.shape[1], row_width),
        "rel",
        split_axis=0,
        concat_axis=0,
        tiled=True,
    )
    ent_grad = jnp.zeros_like(entity).at[send_lists].add(returned)
    neg_share = lax.psum_scatter(grad_neg, "rel", scatter_dimension=0, tiled=True)
    neg_total = lax.psum(neg_share, "dom")
    is_owner = (lax.axis_index("dom") == neg_root).astype(jnp.float32)
    ent_grad = ent_grad.at[neg_rows[rel_here]].add(is_owner * neg_total)
    new_entity, new_entity_acc = adagrad(entity, entity_acc, ent_grad)
    rel_sum = lax.psum(grad_rel, "dom")
    new_relation, new_relation_acc = adagrad(relation, relation_acc, rel_sum)
    return (new_entity, new_entity_acc, new_relation, new_relation_acc)


def solution(mesh):
    in_specs = (
        P(("dom", "rel"), None),
        P(("dom", "rel"), None),
        P("rel", None),
        P("rel", None),
        P(("dom", "rel"), None, None),
        P(("dom", "rel")),
        P(("dom", "rel")),
        P(("dom", "rel")),
        P(),
        P(),
    )
    out_specs = (P(("dom", "rel"), None), P(("dom", "rel"), None), P("rel", None), P("rel", None))
    return jax.shard_map(shards, mesh=mesh, in_specs=in_specs, out_specs=out_specs, check_vma=False)
```

profile of v0, /device:TPU:1, one launch (start us, length us, event | category | flops | bytes accessed | tf_op | source)
XLA Modules:
  0.0 642.0 jit_solution(494855978399194900)
XLA Ops:
  7.2 0.0 all-gather.3.cloned.1.call-start
  7.2 0.7 fusion.40
  8.0 2.2 gather_fusion.3
  10.2 0.0 all-gather.3.cloned.1.call-update
  10.2 0.7 compare_select_fusion.3
  10.9 0.1 copy.14
  11.0 0.1 reshape.123
  11.1 2.3 gather_fusion
  13.4 11.4 %all-to-all-start = ((f32[32,16,512]{2,1,0:T(8,128)}), f32[32,16,512]{2,1,0:T(8,128)S(1)}, u32[]{:S(2)}, u32[]{:S(2)}) async-start(f32[32,16,512]{2,1,0:T(8,128)} %bitcast.1), calls=%async_computation | async-start | bytes 2097152 | tf_op jit(solution)/shard_map/all_to_all | solution.py:62
  24.8 0.0 all-reduce.4.cloned.1.call-start
  25.5 56.8 %all-gather.3.cloned.1.call-done = f32[1024,512]{1,0:T(8,128)} async-done(((f32[32,512]{1,0:T(8,128)}), f32[1024,512]{1,0:T(8,128)}) %all-gather.3.cloned.1.call-update) | async-done | bytes 2097168 | tf_op jit(solution)/shard_map/all_gather | solution.py:68
  82.2 1.6 broadcast_select_fusion
  83.8 0.0 all-reduce.4.cloned.1.call-update
  83.8 0.0 reduce-scatter.2.cloned.1.call-start
  83.9 0.6 copy-done.12
  84.5 0.3 copy-done.1
  84.8 0.4 fusion.24
  85.3 0.2 copy-done.10
  85.5 1.0 gather_fusion.1
  86.4 0.1 multiply_add_fusion.11
  86.5 0.1 multiply_subtract_fusion.3
  86.6 195.2 %all-reduce.4.cloned.1.call-done = f32[1024,512]{1,0:T(8,128)} async-done(((f32[1024,512]{1,0:T(8,128)}), f32[1024,512]{1,0:T(8,128)}) %all-reduce.4.cloned.1.call-update) | async-done | bytes 2097168 | tf_op jit(solution)/shard_map/psum | solution.py:11
  281.8 3.5 fusion.49
  285.4 1.0 copy-done.7
  286.3 3.9 fusion.28
  290.3 0.0 reduce-scatter.2.cloned.1.call-update
  290.3 0.7 copy-done.13
  291.0 1.0 gather_fusion.2
  292.0 0.1 multiply_reduce_fusion
  292.1 0.7 copy-done.3
  292.8 3.1 scatter_custom_fusion
  295.9 4.7 convolution_add_fusion
  300.6 0.1 multiply_add_fusion.9
  300.7 0.1 multiply_add_fusion.7
  300.8 3.1 scatter_custom_fusion.1
  303.9 2.4 add_any.115
  306.4 16.8 %all-to-all-start.1 = ((f32[32,16,512]{2,1,0:T(8,128)}), f32[32,16,512]{2,1,0:T(8,128)S(1)}, u32[]{:S(2)}, u32[]{:S(2)}) async-start(f32[32,16,512]{2,1,0:T(8,128)} %bitcast.6), calls=%async_computation.1 | async-start | bytes 2097152 | tf_op jit(solution)/shard_map/all_to_all | solution.py:76
  323.2 0.0 all-reduce.6.cloned.1.call-start
  323.3 0.1 multiply_add_fusion.4
  323.3 0.1 multiply_add_fusion.5
  323.5 0.4 multiply_negate_fusion
  323.9 0.1 add_multiply_fusion.3
  324.0 0.7 maximum_add_fusion
  324.7 122.2 %reduce-scatter.2.cloned.1.call-done = f32[32,512]{1,0:T(8,128)} async-done(((f32[1024,512]{1,0:T(8,128)}), f32[32,512]{1,0:T(8,128)}) %reduce-scatter.2.cloned.1.call-update) | async-done | bytes 65552 | tf_op jit(solution)/shard_map/reduce_scatter | solution.py:84
  447.0 3.6 scatter_custom_fusion.2
  450.6 181.6 %all-reduce.6.cloned.1.call-done = (f32[32,512]{1,0:T(8,128)}, f32[128,512]{1,0:T(8,128)}) async-done(((f32[32,512]{1,0:T(8,128)}, f32[128,512]{1,0:T(8,128)}), (f32[32,512]{1,0:T(8,128)}, f32[128,512]{1,0:T(8,128)})) %all-reduce.6.cloned.1.call-update) | async-done | bytes 327696 | tf_op jit(solution)/shard_map/psum | solution.py:85
  632.3 1.2 scatter_custom_fusion.3
  633.5 2.0 multiply_subtract_fusion
  (38 shorter events, 0.2 us)
Async XLA Ops:
  7.2 3.9 copy-start
  7.2 75.1 %all-gather.3.cloned.1.call-start = ((), (), s32[]{:S(2)}) async-start(), calls=%async_computation.5 | async-start | bytes 2162688 | tf_op jit(solution)/shard_map/all_gather | solution.py:68
  13.4 71.8 %all-to-all-start = ((f32[32,16,512]{2,1,0:T(8,128)}), f32[32,16,512]{2,1,0:T(8,128)S(1)}, u32[]{:S(2)}, u32[]{:S(2)}) async-start(f32[32,16,512]{2,1,0:T(8,128)} %bitcast.1), calls=%async_computation | async-start | bytes 2097152 | tf_op jit(solution)/shard_map/all_to_all | solution.py:62
  24.8 257.0 %all-reduce.4.cloned.1.call-start = ((), (), s32[]{:S(2)}) async-start(), calls=%async_computation.3 | async-start | bytes 4194304 | tf_op jit(solution)/shard_map/psum | solution.py:11
  83.8 0.7 copy-start.12
  83.8 1.0 copy-start.1
  83.8 1.0 copy-start.14
  83.8 363.1 %reduce-scatter.2.cloned.1.call-start = ((), (), s32[]{:S(2)}) async-start(), calls=%async_computation.4 | async-start | bytes 2162688 | tf_op jit(solution)/shard_map/reduce_scatter | solution.py:84
  84.8 0.6 copy-start.10
  86.5 205.4 %copy-start.4 = (f32[256,128]{1,0:T(8,128)}, f32[256,128]{1,0:T(8,128)S(1)}, u32[]{:S(2)}) copy-start(f32[256,128]{1,0:T(8,128)S(1)} %get-tuple-element.23) | copy-start | bytes 393220
  86.6 205.4 %copy-start.5 = (f32[256,128]{1,0:T(8,128)}, f32[256,128]{1,0:T(8,128)S(1)}, u32[]{:S(2)}) copy-start(f32[256,128]{1,0:T(8,128)S(1)} %get-tuple-element.20) | copy-start | bytes 393220
  86.6 205.4 %copy-start.6 = (f32[256,128]{1,0:T(8,128)}, f32[256,128]{1,0:T(8,128)S(1)}, u32[]{:S(2)}) copy-start(f32[256,128]{1,0:T(8,128)S(1)} %get-tuple-element.21) | copy-start | bytes 393220
  285.3 1.0 copy-start.7
  290.3 0.7 copy-start.13
  292.0 0.8 copy-start.3
  306.3 17.1 %copy-start.2 = (f32[128,512]{1,0:T(8,128)S(1)}, f32[128,512]{1,0:T(8,128)}, u32[]{:S(2)}) copy-start(f32[128,512]{1,0:T(8,128)} %param.12) | copy-start | bytes 786436
  306.3 17.1 %copy-start.11 = (f32[128,128]{1,0:T(8,128)S(1)}, f32[128,128]{1,0:T(8,128)}, u32[]{:S(2)}) copy-start(f32[128,128]{1,0:T(8,128)} %copy-done.10) | copy-start | bytes 196612
  306.4 17.1 %copy-start.15 = (s32[256]{0:T(256)S(1)}, s32[256]{0:T(256)}, u32[]{:S(2)}) copy-start(s32[256]{0:T(256)} %param.16) | copy-start | bytes 3076
  306.4 140.6 %all-to-all-start.1 = ((f32[32,16,512]{2,1,0:T(8,128)}), f32[32,16,512]{2,1,0:T(8,128)S(1)}, u32[]{:S(2)}, u32[]{:S(2)}) async-start(f32[32,16,512]{2,1,0:T(8,128)} %bitcast.6), calls=%async_computation.1 | async-start | bytes 2097152 | tf_op jit(solution)/shard_map/all_to_all | solution.py:76
  323.2 309.1 %all-reduce.6.cloned.1.call-start = ((), (), s32[]{:S(2)}) async-start(), calls=%async_computation.6 | async-start | bytes 655360 | tf_op jit(solution)/shard_map/psum | solution.py:85
  323.4 310.0 %copy-start.8 = (f32[128,512]{1,0:T(8,128)S(1)}, f32[128,512]{1,0:T(8,128)}, u32[]{:S(2)}) copy-start(f32[128,512]{1,0:T(8,128)} %param.13) | copy-start | bytes 786436
  323.5 310.0 %copy-start.9 = (f32[128,512]{1,0:T(8,128)S(1)}, f32[128,512]{1,0:T(8,128)}, u32[]{:S(2)}) copy-start(f32[128,512]{1,0:T(8,128)} %param.11) | copy-start | bytes 786436
Sparse Core Ops, SparseCore 0:
  10.7 71.4 all-gather.2
  85.2 196.6 all-reduce.3
  290.4 156.4 reduce-scatter.1
  450.3 181.8 all-reduce.5
where the time goes:
time: 653 us; the launch traced here: 642 us
  waiting for transfers between devices  556 us (85%)
  starting transfers between devices  28.4 us (4%)
  other arithmetic  20 us (3%)
  between operations  14.7 us (2%)
  matrix products  13 us (2%)
  local copies, waits for them, and re-layouts  10.1 us (2%)
    psum x1, waiting for transfers between devices, broadcast(): return lax.psum(block, axis)  195 us
    psum x1, waiting for transfers between devices, shards(): neg_total = lax.psum(neg_share, 'dom')  182 us
    reduce_scatter x1, waiting for transfers between devices, shards(): lax.psum_scatter(grad_neg, 'rel', scatter_dimension=0, tiled=True)  122 us
    all_gather x1, waiting for transfers between devices, shards(): grouped = lax.all_gather(own_negs, 'rel', axis=0, tiled=True)  56.8 us
    all_to_all x1, starting transfers between devices, shards(): lax.all_to_all(grad_rows.reshape(-1, send_lists.shape[1], row_width), 're...  16.8 us
  transfers between devices with their start and end apart: 6, of which 4 were waited for; matrix products, arithmetic and copies ran while one was open for 4% of the time, Pallas kernels for 0%

commit v1 on v0

v1 whole, which is shorter than its diff:
```python
import jax
import jax.numpy as jnp
from jax import lax
from jax.experimental import pallas as pl
from jax.experimental.pallas import tpu as pltpu
from jax.sharding import PartitionSpec as P

MESH = pl.DeviceIdType.MESH
F32, BF16 = jnp.float32, jnp.bfloat16
step_size = 0.05

N_DOM, N_REL = 16, 32
NY, NX = 8, 4
ZX = 32
ENT, RELS, TRIP, SLOTS, NEG, WIDTH = 128, 128, 256, 16, 32, 512
TILE = (8, 128)
NEGS = NEG * N_REL

NN = (((1,), (0,)), ((), ()))
TN = (((0,), (0,)), ((), ()))
NT = (((1,), (1,)), ((), ()))


def mm(a, b, dims):
    return lax.dot_general(a, b, dims, preferred_element_type=F32)


def halves(v):
    hi = v.astype(BF16)
    return hi, (v - hi.astype(F32)).astype(BF16)


def select(one_hot, v, dims):
    hi, lo = halves(v)
    return mm(one_hot, hi, dims) + mm(one_hot, lo, dims)


def mm3(a, b, dims):
    return mm(a[0], b[0], dims) + (mm(a[0], b[1], dims) + mm(a[1], b[0], dims))


def hot(rows, index_row):
    n = index_row.shape[1]
    at = lax.broadcasted_iota(jnp.int32, (rows, n), 0)
    return jnp.where(at == index_row, 1.0, 0.0).astype(BF16)


def rcopy(src, dst, ssem, rsem, dev):
    return pltpu.make_async_remote_copy(
        src_ref=src, dst_ref=dst, send_sem=ssem, recv_sem=rsem, device_id=dev, device_id_type=MESH
    )


def quarter(v):
    return v[:, 0:128], v[:, 128:256], v[:, 256:384], v[:, 384:512]


def adagrad(values, history, gradient):
    history_new = history + gradient * gradient
    return values - step_size * gradient / jnp.sqrt(history_new), history_new


def kernel(
    entity, entity_acc, relation, relation_acc, send_row, ends_row, rels_row, neg_rows, neg_part,
    new_e, new_ea, new_r, new_ra,
    send_buf, recv, neg_src, s1_recv, nbuf, hot_ends, ends, rot, query, dq, dends,
    gall, xrecv, ring, rp, rm, zx_recv, relx, tile_out, t_recv, rel_full, gt, ret,
    a_s, a_r, b_s, b_r, s1_s, s1_r, s2_s, s2_r, yp_s, yp_r, ym_s, ym_r, sib_s, sib_r, x_s, x_r,
    rp_s, rp_r, rm_s, rm_r, z_s, z_r, rx_s, rx_r, t_s, t_r, ra_s, ra_r,
):
    dom, rel = lax.axis_index("dom"), lax.axis_index("rel")
    zh, y = lax.div(dom, NY), lax.rem(dom, NY)
    zx_low, core = lax.div(rel, 2), lax.rem(rel, 2)
    zi = zh * 16 + zx_low
    root = neg_part[0]
    up, down = lax.rem(y + 1, NY), lax.rem(y + NY - 1, NY)
    up_dev, down_dev = {"dom": zh * NY + up}, {"dom": zh * NY + down}
    sib_dev = {"rel": zx_low * 2 + (1 - core)}

    def zx_dev(p):
        return {"dom": lax.div(p, 16) * NY + y, "rel": lax.rem(p, 16) * 2 + core}

    barrier = pltpu.get_barrier_semaphore()

    @pl.loop(1, N_DOM)
    def _(k):
        pl.semaphore_signal(
            barrier, inc=1, device_id={"dom": lax.rem(dom + k, N_DOM)}, device_id_type=MESH
        )

    @pl.loop(1, N_REL)
    def _(k):
        pl.semaphore_signal(
            barrier, inc=1, device_id={"rel": lax.rem(rel + k, N_REL)}, device_id_type=MESH
        )

    @pl.loop(1, 16)
    def _(k):
        p = (1 - zh) * 16 + lax.rem(zx_low + k, 16)
        pl.semaphore_signal(barrier, inc=1, device_id=zx_dev(p), device_id_type=MESH)

    ent = entity[...]
    neg_hot = hot(ENT, neg_rows[pl.ds(rel, 1), :])
    own = select(neg_hot, ent, TN)
    for g in range(4):
        for w in range(4):
            neg_src[g * 4 + w] = own[g * 8 : g * 8 + 8, w * 128 : w * 128 + 128]
    send_hot = hot(ENT, send_row[...])
    send_buf[...] = select(send_hot, ent, TN).reshape(N_REL, SLOTS, WIDTH)

    pl.semaphore_wait(barrier, (N_DOM - 1) + (N_REL - 1) + 15)

    @pl.loop(1, N_DOM)
    def _(k):
        p = lax.rem(dom + k, N_DOM)
        rcopy(neg_src.at[p], s1_recv.at[dom], s1_s.at[k], s1_r.at[dom], {"dom": p}).start()

    def exchange(src, dst, ssem, rsem, k):
        p = lax.rem(rel + k, N_REL)
        rcopy(src.at[p], dst.at[rel], ssem.at[k], rsem.at[rel], {"rel": p}).start()

    @pl.loop(16, N_REL)
    def _(k):
        exchange(send_buf, recv, a_s, a_r, k)

    s1_recv[dom] = neg_src[dom]
    recv[rel] = send_buf[rel]

    @pl.loop(1, N_DOM)
    def _(k):
        p = lax.rem(dom + k, N_DOM)
        rcopy(neg_src.at[p], s1_recv.at[p], s1_s.at[k], s1_r.at[p], {"dom": p}).wait_recv()

    mine = core * NY + y
    nbuf[mine, zi] = s1_recv[root]

    @pl.loop(1, ZX)
    def _(k):
        p = lax.rem(zi + k, ZX)
        here = nbuf.at[mine, zi]
        rcopy(here, here, s2_s.at[k], s2_r.at[zi], zx_dev(p)).start()

    @pl.loop(1, 16)
    def _(k):
        exchange(send_buf, recv, a_s, a_r, k)

    @pl.loop(1, ZX)
    def _(k):
        p = lax.rem(zi + k, ZX)
        there = nbuf.at[mine, p]
        rcopy(there, there, s2_s.at[k], s2_r.at[p], zx_dev(p)).wait_recv()

    def block(yy):
        return nbuf.at[core * NY + lax.rem(yy + 2 * NY, NY)]

    def part(yy, lo):
        return nbuf.at[core * NY + lax.rem(yy + 2 * NY, NY), pl.ds(lo, ZX // 2)]

    def pass_up(ref, n):
        return rcopy(ref, ref, yp_s.at[n], yp_r.at[n], up_dev)

    def pass_down(ref, n):
        return rcopy(ref, ref, ym_s.at[n], ym_r.at[n], down_dev)

    def to_sib(ref, n):
        return rcopy(ref, ref, sib_s.at[n], sib_r.at[n], sib_dev)

    sent = [pass_up(block(y), 0), pass_down(block(y), 0), to_sib(block(y), 0)]
    for c in sent:
        c.start()
    for n in (1, 2):
        pass_up(block(y - n), n - 1).wait_recv()
        nxt = [pass_up(block(y - n), n), to_sib(block(y - n), 2 * n - 1)]
        for c in nxt:
            c.start()
        sent += nxt
        pass_down(block(y + n), n - 1).wait_recv()
        nxt = [pass_down(block(y + n), n), to_sib(block(y + n), 2 * n)]
        for c in nxt:
            c.start()
        sent += nxt
    half = ZX // 2
    pass_up(block(y - 3), 2).wait_recv()
    nxt = [pass_up(part(y - 3, 0), 3), to_sib(block(y - 3), 5)]
    for c in nxt:
        c.start()
    sent += nxt
    pass_down(block(y + 3), 2).wait_recv()
    nxt = [pass_down(part(y + 3, half), 3), to_sib(block(y + 3), 6)]
    for c in nxt:
        c.start()
    sent += nxt

    @pl.loop(1, N_REL)
    def _(k):
        p = lax.rem(rel + k, N_REL)
        rcopy(send_buf.at[p], recv.at[p], a_s.at[k], a_r.at[p], {"rel": p}).wait_recv()

    hot_ends[...] = hot(N_REL * SLOTS, ends_row[...])
    ends[...] = select(hot_ends[...], recv[...].reshape(N_REL * SLOTS, WIDTH), TN)
    rel_hot = hot(RELS, rels_row[...])
    ra, rb, rc, rd = quarter(relation[...])
    inv = 1.0 / jnp.sqrt(ra * ra + rb * rb + rc * rc + rd * rd)
    unit = jnp.concatenate([ra * inv, rb * inv, rc * inv, rd * inv], axis=1)
    rot[...] = select(rel_hot, unit, TN)
    ha, hb, hc, hd = quarter(ends[pl.ds(0, TRIP), :])
    ua, ub, uc, ud = quarter(rot[...])
    qa = ha * ua - hb * ub - hc * uc - hd * ud
    qb = ha * ub + hb * ua + hc * ud - hd * uc
    qc = ha * uc - hb * ud + hc * ua + hd * ub
    qd = ha * ud + hb * uc - hc * ub + hd * ua
    query[...] = jnp.concatenate([qa, qb, qc, qd], axis=1)
    tails = ends[pl.ds(TRIP, TRIP), :]
    positive = jnp.sum(query[...] * tails, axis=1, keepdims=True)
    pull = -1.0 / (1.0 + jnp.exp(positive))
    dq[...] = pull * tails
    dends[pl.ds(TRIP, TRIP), :] = pull * query[...]

    pass_up(part(y - 4, 0), 3).wait_recv()
    nxt = [to_sib(part(y - 4, 0), 7)]
    nxt[0].start()
    sent += nxt
    pass_down(part(y + 4, half), 3).wait_recv()
    nxt = [to_sib(part(y + 4, half), 8)]
    nxt[0].start()
    sent += nxt

    def sib_block(yy):
        return nbuf.at[(1 - core) * NY + lax.rem(yy + 2 * NY, NY)]

    def sib_part(yy, lo):
        return nbuf.at[(1 - core) * NY + lax.rem(yy + 2 * NY, NY), pl.ds(lo, half)]

    to_sib(sib_block(y), 0).wait_recv()
    for n in (1, 2, 3):
        to_sib(sib_block(y - n), 2 * n - 1).wait_recv()
        to_sib(sib_block(y + n), 2 * n).wait_recv()
    to_sib(sib_part(y - 4, 0), 7).wait_recv()
    to_sib(sib_part(y + 4, half), 8).wait_recv()

    @pl.loop(0, 4)
    def _(b):
        q = halves(query[...])
        n = halves(
            jnp.concatenate(
                [nbuf[b * 4 + w].reshape(ZX * 8, 128) for w in range(4)], axis=1
            )
        )
        s = mm3(q, n, NT)
        p = halves((1.0 / NEGS) / (1.0 + jnp.exp(-s)))
        dq[...] += mm3(p, n, NN)
        dn = mm3(p, q, TN)
        for w in range(4):
            gall[b * 4 + w] = dn[:, w * 128 : w * 128 + 128].reshape(ZX, 8, 128)

    swap = rcopy(gall.at[pl.ds((1 - core) * NY, NY)], xrecv, x_s, x_r, sib_dev)
    swap.start()
    sent.append(swap)

    ga, gb, gc, gd = quarter(dq[...])
    ha, hb, hc, hd = quarter(ends[pl.ds(0, TRIP), :])
    ua, ub, uc, ud = quarter(rot[...])
    dha = ga * ua + gb * ub + gc * uc + gd * ud
    dhb = gb * ua - ga * ub - gc * ud + gd * uc
    dhc = gb * ud - ga * uc + gc * ua - gd * ub
    dhd = gc * ub - ga * ud - gb * uc + gd * ua
    dends[pl.ds(0, TRIP), :] = jnp.concatenate([dha, dhb, dhc, dhd], axis=1)
    gt[...] = select(hot_ends[...], dends[...], NN).reshape(N_REL, SLOTS, WIDTH)

    @pl.loop(16, N_REL)
    def _(k):
        exchange(gt, ret, b_s, b_r, k)

    @pl.loop(1, 16)
    def _(k):
        exchange(gt, ret, b_s, b_r, k)

    ret[rel] = gt[rel]
    dua = ga * ha + gb * hb + gc * hc + gd * hd
    dub = gb * ha - ga * hb + gc * hd - gd * hc
    duc = gc * ha - ga * hc - gb * hd + gd * hb
    dud = gb * hc - ga * hd - gc * hb + gd * ha
    rel_hot = hot(RELS, rels_row[...])
    du = select(rel_hot, jnp.concatenate([dua, dub, duc, dud], axis=1), NN)
    ra, rb, rc, rd = quarter(relation[...])
    inv = 1.0 / jnp.sqrt(ra * ra + rb * rb + rc * rc + rd * rd)
    va, vb, vc, vd = ra * inv, rb * inv, rc * inv, rd * inv
    da, db, dc, dd = quarter(du)
    along = da * va + db * vb + dc * vc + dd * vd
    parts = [(g - v * along) * inv for g, v in ((da, va), (db, vb), (dc, vc), (dd, vd))]
    for yy in range(NY):
        for g in range(2):
            for w in range(4):
                at = yy * 16 + g * 8
                ring[yy, ZX + g * 4 + w] = parts[w][at : at + 8, :]

    rcopy(gall.at[pl.ds(core * NY, NY)], xrecv, x_s, x_r, sib_dev).wait_recv()

    @pl.loop(0, NY)
    def _(k):
        ring[k, pl.ds(0, ZX)] = gall[core * NY + k] + xrecv[k]

    def chunk(yy, lo, n):
        return ring.at[lax.rem(yy + 2 * NY, NY), pl.ds(lo, n)]

    def add_up(yy, lo, n, got):
        i = lax.rem(yy + 2 * NY, NY)
        ring[i, pl.ds(lo, n)] = ring[i, pl.ds(lo, n)] + got[pl.ds(lo, n)]

    def sum_up(yy, lo, n, s):
        return rcopy(chunk(yy, lo, n), rp.at[s, pl.ds(lo, n)], rp_s.at[s], rp_r.at[s], up_dev)

    def sum_down(yy, lo, n, s):
        return rcopy(chunk(yy, lo, n), rm.at[s, pl.ds(lo, n)], rm_s.at[s], rm_r.at[s], down_dev)

    nxt = [sum_up(y + 4, 0, 20, 0), sum_down(y - 4, 20, 20, 0)]
    for c in nxt:
        c.start()
    sent += nxt
    for s in (1, 2, 3):
        lo_u, n_u, lo_d, n_d = (0, 20, 20, 20) if s == 1 else (0, 40, 0, 40)
        sum_up(y + 4 - s, lo_u, n_u, s - 1).wait_recv()
        add_up(y + 4 - s, lo_u, n_u, rp.at[s - 1])
        c = sum_up(y + 4 - s, 0, 40, s)
        c.start()
        sent.append(c)
        sum_down(y - 4 + s, lo_d, n_d, s - 1).wait_recv()
        add_up(y - 4 + s, lo_d, n_d, rm.at[s - 1])
        c = sum_down(y - 4 + s, 0, 40, s)
        c.start()
        sent.append(c)
    sum_up(y, 0, 40, 3).wait_recv()
    sum_down(y, 0, 40, 3).wait_recv()
    ring[y] = ring[y] + (rp[3] + rm[3])

    far = {"dom": (1 - zh) * NY + y}
    cross = rcopy(ring.at[y, pl.ds(ZX, 8)], relx, rx_s, rx_r, far)
    cross.start()
    sent.append(cross)

    @pl.loop(1, ZX)
    def _(k):
        p = lax.rem(zi + k, ZX)
        rcopy(ring.at[y, p], zx_recv.at[zi], z_s.at[k], z_r.at[zi], zx_dev(p)).start()

    zx_recv[zi] = ring[y, zi]

    @pl.loop(1, ZX)
    def _(k):
        p = lax.rem(zi + k, ZX)
        rcopy(ring.at[y, p], zx_recv.at[p], z_s.at[k], z_r.at[p], zx_dev(p)).wait_recv()

    tile_out[...] = jnp.sum(zx_recv[...], axis=0)

    @pl.loop(1, N_DOM)
    def _(k):
        p = lax.rem(dom + k, N_DOM)
        rcopy(tile_out, t_recv.at[dom], t_s.at[k], t_r.at[dom], {"dom": p}).start()

    t_recv[dom] = tile_out[...]
    cross.wait_recv()
    rel_full[y] = ring[y, pl.ds(ZX, 8)] + relx[...]

    @pl.loop(1, NY)
    def _(k):
        to = {"dom": zh * NY + lax.rem(y + k, NY)}
        rcopy(rel_full.at[y], rel_full.at[y], ra_s.at[k], ra_r.at[y], to).start()

    @pl.loop(1, N_REL)
    def _(k):
        p = lax.rem(rel + k, N_REL)
        rcopy(gt.at[p], ret.at[p], b_s.at[k], b_r.at[p], {"rel": p}).wait_recv()

    send_hot = hot(ENT, send_row[...])
    grad = select(send_hot, ret[...].reshape(N_REL * SLOTS, WIDTH), NN)

    @pl.loop(1, N_DOM)
    def _(k):
        p = lax.rem(dom + k, N_DOM)
        rcopy(tile_out, t_recv.at[p], t_s.at[k], t_r.at[p], {"dom": p}).wait_recv()

    total = jnp.concatenate(
        [
            jnp.concatenate([t_recv[g * 4 + w] for w in range(4)], axis=1)
            for g in range(4)
        ],
        axis=0,
    )
    owner = jnp.where(dom == root, 1.0, 0.0).astype(F32)
    neg_hot = hot(ENT, neg_rows[pl.ds(rel, 1), :])
    grad = grad + owner * select(neg_hot, total, NN)
    e, ea = adagrad(entity[...], entity_acc[...], grad)
    new_e[...] = e
    new_ea[...] = ea

    @pl.loop(1, NY)
    def _(k):
        i = lax.rem(y + k, NY)
        there = rel_full.at[i]
        rcopy(there, there, ra_s.at[k], ra_r.at[i], {"dom": zh * NY + i}).wait_recv()

    for w in range(4):
        cols = pl.ds(w * 128, 128)
        g = jnp.concatenate(
            [rel_full[yy, gg * 4 + w] for yy in range(NY) for gg in range(2)], axis=0
        )
        r, racc = adagrad(relation[:, cols], relation_acc[:, cols], g)
        new_r[:, cols] = r
        new_ra[:, cols] = racc

    for c in sent:
        c.wait_send()

    @pl.loop(1, N_DOM)
    def _(k):
        p = lax.rem(dom + k, N_DOM)
        rcopy(neg_src.at[p], s1_recv.at[dom], s1_s.at[k], s1_r.at[dom], {"dom": p}).wait_send()
        rcopy(tile_out, t_recv.at[dom], t_s.at[k], t_r.at[dom], {"dom": p}).wait_send()

    @pl.loop(1, N_REL)
    def _(k):
        p = lax.rem(rel + k, N_REL)
        rcopy(send_buf.at[p], recv.at[rel], a_s.at[k], a_r.at[rel], {"rel": p}).wait_send()
        rcopy(gt.at[p], ret.at[rel], b_s.at[k], b_r.at[rel], {"rel": p}).wait_send()

    @pl.loop(1, ZX)
    def _(k):
        p = lax.rem(zi + k, ZX)
        here = nbuf.at[mine, zi]
        rcopy(here, here, s2_s.at[k], s2_r.at[zi], zx_dev(p)).wait_send()
        rcopy(ring.at[y, p], zx_recv.at[zi], z_s.at[k], z_r.at[zi], zx_dev(p)).wait_send()

    @pl.loop(1, NY)
    def _(k):
        to = {"dom": zh * NY + lax.rem(y + k, NY)}
        rcopy(rel_full.at[y], rel_full.at[y], ra_s.at[k], ra_r.at[y], to).wait_send()


def shards(
    entity, entity_acc, relation, relation_acc, send_rows, trip_head, trip_rel, trip_tail, neg_part, neg_rows,
):
    send_row = send_rows.reshape(1, N_REL * SLOTS)
    ends_row = jnp.concatenate([trip_head, trip_tail]).reshape(1, 2 * TRIP)
    rels_row = trip_rel.reshape(1, TRIP)
    vmem = pl.BlockSpec(memory_space=pltpu.VMEM)
    smem = pl.BlockSpec(memory_space=pltpu.SMEM)
    dma = pltpu.SemaphoreType.DMA
    rows = jax.ShapeDtypeStruct((ENT, WIDTH), F32)
    return pl.pallas_call(
        kernel,
        out_shape=(rows, rows, rows, rows),
        in_specs=[vmem] * 8 + [smem],
        out_specs=(vmem,) * 4,
        scratch_shapes=[
            pltpu.VMEM((N_REL, SLOTS, WIDTH), F32),
            pltpu.VMEM((N_REL, SLOTS, WIDTH), F32),
            pltpu.VMEM((N_DOM, *TILE), F32),
            pltpu.VMEM((N_DOM, *TILE), F32),
            pltpu.VMEM((2 * NY, ZX, *TILE), F32),
            pltpu.VMEM((N_REL * SLOTS, 2 * TRIP), BF16),
            pltpu.VMEM((2 * TRIP, WIDTH), F32),
            pltpu.VMEM((TRIP, WIDTH), F32),
            pltpu.VMEM((TRIP, WIDTH), F32),
            pltpu.VMEM((TRIP, WIDTH), F32),
            pltpu.VMEM((2 * TRIP, WIDTH), F32),
            pltpu.VMEM((2 * NY, ZX, *TILE), F32),
            pltpu.VMEM((NY, ZX, *TILE), F32),
            pltpu.VMEM((NY, ZX + 8, *TILE), F32),
            pltpu.VMEM((4, ZX + 8, *TILE), F32),
            pltpu.VMEM((4, ZX + 8, *TILE), F32),
            pltpu.VMEM((ZX, *TILE), F32),
            pltpu.VMEM((8, *TILE), F32),
            pltpu.VMEM(TILE, F32),
            pltpu.VMEM((N_DOM, *TILE), F32),
            pltpu.VMEM((NY, 8, *TILE), F32),
            pltpu.VMEM((N_REL, SLOTS, WIDTH), F32),
            pltpu.VMEM((N_REL, SLOTS, WIDTH), F32),
            dma((N_REL,)), dma((N_REL,)), dma((N_REL,)), dma((N_REL,)),
            dma((N_DOM,)), dma((N_DOM,)), dma((ZX,)), dma((ZX,)),
            dma((4,)), dma((4,)), dma((4,)), dma((4,)),
            dma((9,)), dma((9,)), dma, dma,
            dma((4,)), dma((4,)), dma((4,)), dma((4,)),
            dma((ZX,)), dma((ZX,)), dma, dma,
            dma((N_DOM,)), dma((N_DOM,)), dma((NY,)), dma((NY,)),
        ],
        compiler_params=pltpu.CompilerParams(
            collective_id=0, has_side_effects=True, vmem_limit_bytes=56 << 20
        ),
        name="step",
    )(entity, entity_acc, relation, relation_acc, send_row, ends_row, rels_row, neg_rows, neg_part)


def solution(mesh):
    both = ("dom", "rel")
    in_specs = (
        P(both, None), P(both, None), P("rel", None), P("rel", None), P(both, None, None),
        P(both), P(both), P(both), P(), P(),
    )
    out_specs = (P(both, None), P(both, None), P("rel", None), P("rel", None))
    return jax.shard_map(shards, mesh=mesh, in_specs=in_specs, out_specs=out_specs, check_vma=False)
```

time: 653 us -> 125 us (0.19); the launches traced: 642 us -> 125 us
  waiting for transfers between devices: 556 us -> 0 us
  Pallas kernels: 0 us -> 117 us
  starting transfers between devices: 28.4 us -> 0 us
  other arithmetic: 20 us -> 1.28 us
  between operations: 14.7 us -> 1.32 us
  matrix products: 13 us -> 0 us
    psum x2 -> x0, waiting for transfers between devices: 377 us -> none  [the longest x1 195 us: broadcast(): return lax.psum(block, axis)]
    reduce_scatter x1 -> x0, waiting for transfers between devices: 122 us -> none  [shards(): lax.psum_scatter(grad_neg, 'rel', scatter_dimension=0, tiled=True)]
    pallas_call x0 -> x1, Pallas kernels: none -> 117 us  [shards(): pl.pallas_call(kernel, out_shape=(rows, rows, rows, rows), in_specs=[vmem...]
    all_gather x1 -> x0, waiting for transfers between devices: 56.8 us -> none  [shards(): grouped = lax.all_gather(own_negs, 'rel', axis=0, tiled=True)]
    all_to_all x2 -> x0, starting transfers between devices: 28.2 us -> none  [the longest x1 16.8 us: shards(): lax.all_to_all(grad_rows.reshape(-1, send_lists.shape[1], row_width), 're...]
    dot_general x5 -> x0, matrix products: 13 us -> none  [the longest x3 12.2 us: local_loss(): jnp.einsum('ik,jk->ij', query, negatives, precision=lax.Precision.HIGHEST)]
    scatter-add x4 -> x0, other arithmetic: 11.1 us -> none  [the longest x1 3.65 us: shards(): ent_grad = jnp.zeros_like(entity).at[send_lists].add(returned)]
  transfers between devices with their start and end apart: 6 -> 0, of which waited for: 4 -> 0; matrix products, arithmetic and copies ran while one was open for 4% -> 0% of each run, Pallas kernels for 0% -> 0%
where the time goes in v1:
time: 125 us
  Pallas kernels  117 us (94%)
  local copies, waits for them, and re-layouts  5.25 us (4%)
  between operations  1.32 us (1%)
  other arithmetic  1.28 us (1%)
    pallas_call x1, Pallas kernels, shards(): pl.pallas_call(kernel, out_shape=(rows, rows, rows, rows), in_specs=[vmem...  117 us
    unnamed x13, local copies, waits for them, and re-layouts  4.58 us

profile of v1, /device:TPU:1, one launch (start us, length us, event | category | flops | bytes accessed | tf_op | source)
XLA Modules:
  0.0 124.8 jit_solution(14635849082921678767)
XLA Ops:
  0.6 0.0 copy-start.3
  1.3 1.3 %pad_add_fusion = s32[512]{0:T(512)} fusion(s32[256]{0:T(256)} %param.17, s32[256]{0:T(256)} %param.15), kind=kLoop, calls=%fused_computation | loop fusion | flops 512 | bytes 4096 | tf_op jit(solution)/shard_map/concatenate | solution.py:443
  2.6 0.0 copy-done.3
  2.6 0.1 copy.15
  2.7 0.7 reshape.17.send_row
  3.3 117.0 %step.1 = (f32[128,512]{1,0:T(8,128)}, f32[128,512]{1,0:T(8,128)}, f32[128,512]{1,0:T(8,128)}, f32[128,512]{1,0:T(8,128)}) custom-call(f32[128,512]{1,0:T(8,128)} %entity.1, f32[128,512]{1,0:T(8,128)} %entity_acc.1, f32[128,512]{1,0:T(8,128)} %relation.1, f32[128,512]{1,0:T(8,128)} %relation_acc.1, s32[1,512]{1,0:T(1,128)} %reshape.17.send_row, ...), custom_call_target="tpu_custom_call" | custom-call | tf_op jit(solution)/shard_map/step/pallas_call | solution.py:449
  120.3 0.0 copy-start.2
  120.3 1.7 %copy.21 = f32[128,512]{1,0:T(8,128)} copy(f32[128,512]{1,0:T(8,128)} %get-tuple-element.8) | data formatting | bytes 524288
  122.0 0.0 copy-done.2
  122.0 0.0 copy-start.1
  122.0 0.7 copy.22
  122.7 0.3 copy-done.1
  123.1 0.0 copy-start
  123.1 0.7 copy.23
  123.8 0.3 copy-done
  124.1 0.7 copy.24
Async XLA Ops:
  0.6 2.0 %copy-start.3 = (s32[1,32,16]{1,2,0:T(8,128)S(1)}, s32[1,32,16]{1,2,0:T(8,128)}, u32[]{:S(2)}) copy-start(s32[1,32,16]{1,2,0:T(8,128)} %param.14) | copy-start | bytes 6148
  120.3 1.7 %copy-start.2 = (f32[128,512]{1,0:T(8,128)S(1)}, f32[128,512]{1,0:T(8,128)}, u32[]{:S(2)}) copy-start(f32[128,512]{1,0:T(8,128)} %get-tuple-element.9) | copy-start | bytes 786436
  122.0 1.0 copy-start.1
  123.1 1.0 copy-start

commit v2 on v1

--- a/solution.py
+++ b/solution.py
@@ -15,6 +15,9 @@
 ENT, RELS, TRIP, SLOTS, NEG, WIDTH = 128, 128, 256, 16, 32, 512
 TILE = (8, 128)
 NEGS = NEG * N_REL
+FIRST = 24
+HALF = ZX // 2
+CUT = 20
 
 NN = (((1,), (0,)), ((), ()))
 TN = (((0,), (0,)), ((), ()))
@@ -45,6 +48,18 @@
     return jnp.where(at == index_row, 1.0, 0.0).astype(BF16)
 
 
+def slot_row(send_t):
+    n = N_REL * SLOTS
+    at = lax.broadcasted_iota(jnp.int32, (N_REL, n), 1)
+    spread = lax.div(at, SLOTS) == lax.broadcasted_iota(jnp.int32, (N_REL, n), 0)
+    full = mm(
+        send_t[...].astype(F32).astype(BF16), jnp.where(spread, 1.0, 0.0).astype(BF16), NN
+    )
+    slot = lax.rem(lax.broadcasted_iota(jnp.int32, (SLOTS, n), 1), SLOTS)
+    keep = slot == lax.broadcasted_iota(jnp.int32, (SLOTS, n), 0)
+    return jnp.sum(jnp.where(keep, full, 0.0), axis=0, keepdims=True).astype(jnp.int32)
+
+
 def rcopy(src, dst, ssem, rsem, dev):
     return pltpu.make_async_remote_copy(
         src_ref=src, dst_ref=dst, send_sem=ssem, recv_sem=rsem, device_id=dev, device_id_type=MESH
@@ -61,18 +76,29 @@
 
 
 def kernel(
-    entity, entity_acc, relation, relation_acc, send_row, ends_row, rels_row, neg_rows, neg_part,
-    new_e, new_ea, new_r, new_ra,
+    entity_h, relation_h, send_h, head_h, tail_h, rels_h, neg_h, part_h,
+    grad_e, grad_r,
+    entity, relation, send_t, head_row, tail_row, rels_row, neg_rows, neg_part,
     send_buf, recv, neg_src, s1_recv, nbuf, hot_ends, ends, rot, query, dq, dends,
     gall, xrecv, ring, rp, rm, zx_recv, relx, tile_out, t_recv, rel_full, gt, ret,
-    a_s, a_r, b_s, b_r, s1_s, s1_r, s2_s, s2_r, yp_s, yp_r, ym_s, ym_r, sib_s, sib_r, x_s, x_r,
+    in_s, a_s, a_r, b_s, b_r, s1_s, s1_r, s2_s, s2_r, yp_s, yp_r, ym_s, ym_r, sib_s, sib_r, x_s, x_r,
     rp_s, rp_r, rm_s, rm_r, z_s, z_r, rx_s, rx_r, t_s, t_r, ra_s, ra_r,
 ):
+    loads = [
+        pltpu.make_async_copy(h, v, in_s.at[n])
+        for n, (h, v) in enumerate(
+            (
+                (entity_h, entity), (neg_h, neg_rows), (send_h, send_t), (part_h, neg_part),
+                (head_h, head_row), (tail_h, tail_row), (rels_h, rels_row), (relation_h, relation),
+            )
+        )
+    ]
+    for c in loads:
+        c.start()
     dom, rel = lax.axis_index("dom"), lax.axis_index("rel")
     zh, y = lax.div(dom, NY), lax.rem(dom, NY)
     zx_low, core = lax.div(rel, 2), lax.rem(rel, 2)
     zi = zh * 16 + zx_low
-    root = neg_part[0]
     up, down = lax.rem(y + 1, NY), lax.rem(y + NY - 1, NY)
     up_dev, down_dev = {"dom": zh * NY + up}, {"dom": zh * NY + down}
     sib_dev = {"rel": zx_low * 2 + (1 - core)}
@@ -99,14 +125,20 @@
         p = (1 - zh) * 16 + lax.rem(zx_low + k, 16)
         pl.semaphore_signal(barrier, inc=1, device_id=zx_dev(p), device_id_type=MESH)
 
-    ent = entity[...]
+    for c in loads[:4]:
+        c.wait()
+    ent = halves(entity[...])
     neg_hot = hot(ENT, neg_rows[pl.ds(rel, 1), :])
-    own = select(neg_hot, ent, TN)
+    own = mm(neg_hot, ent[0], TN) + mm(neg_hot, ent[1], TN)
     for g in range(4):
         for w in range(4):
             neg_src[g * 4 + w] = own[g * 8 : g * 8 + 8, w * 128 : w * 128 + 128]
-    send_hot = hot(ENT, send_row[...])
-    send_buf[...] = select(send_hot, ent, TN).reshape(N_REL, SLOTS, WIDTH)
+    send_hot = hot(ENT, slot_row(send_t))
+    rows = mm(send_hot, ent[0], TN) + mm(send_hot, ent[1], TN)
+    send_buf[...] = rows.reshape(N_REL, SLOTS, WIDTH)
+    for c in loads[4:]:
+        c.wait()
+    is_root = lax.broadcasted_iota(jnp.int32, (N_DOM, 1, 1), 0) == neg_part[...].reshape(1, 1, 1)
 
     pl.semaphore_wait(barrier, (N_DOM - 1) + (N_REL - 1) + 15)
 
@@ -119,7 +151,7 @@
         p = lax.rem(rel + k, N_REL)
         rcopy(src.at[p], dst.at[rel], ssem.at[k], rsem.at[rel], {"rel": p}).start()
 
-    @pl.loop(16, N_REL)
+    @pl.loop(FIRST, N_REL)
     def _(k):
         exchange(send_buf, recv, a_s, a_r, k)
 
@@ -132,7 +164,7 @@
         rcopy(neg_src.at[p], s1_recv.at[p], s1_s.at[k], s1_r.at[p], {"dom": p}).wait_recv()
 
     mine = core * NY + y
-    nbuf[mine, zi] = s1_recv[root]
+    nbuf[mine, zi] = jnp.sum(jnp.where(is_root, s1_recv[...], 0.0), axis=0)
 
     @pl.loop(1, ZX)
     def _(k):
@@ -140,7 +172,7 @@
         here = nbuf.at[mine, zi]
         rcopy(here, here, s2_s.at[k], s2_r.at[zi], zx_dev(p)).start()
 
-    @pl.loop(1, 16)
+    @pl.loop(1, FIRST)
     def _(k):
         exchange(send_buf, recv, a_s, a_r, k)
 
@@ -150,53 +182,51 @@
         there = nbuf.at[mine, p]
         rcopy(there, there, s2_s.at[k], s2_r.at[p], zx_dev(p)).wait_recv()
 
-    def block(yy):
-        return nbuf.at[core * NY + lax.rem(yy + 2 * NY, NY)]
-
-    def part(yy, lo):
-        return nbuf.at[core * NY + lax.rem(yy + 2 * NY, NY), pl.ds(lo, ZX // 2)]
-
-    def pass_up(ref, n):
-        return rcopy(ref, ref, yp_s.at[n], yp_r.at[n], up_dev)
-
-    def pass_down(ref, n):
-        return rcopy(ref, ref, ym_s.at[n], ym_r.at[n], down_dev)
-
-    def to_sib(ref, n):
-        return rcopy(ref, ref, sib_s.at[n], sib_r.at[n], sib_dev)
-
-    sent = [pass_up(block(y), 0), pass_down(block(y), 0), to_sib(block(y), 0)]
-    for c in sent:
+    def part(core_of, yy, h):
+        return nbuf.at[core_of * NY + lax.rem(yy + 2 * NY, NY), pl.ds(h * HALF, HALF)]
+
+    def pass_up(yy, h, n):
+        ref = part(core, yy, h)
+        return rcopy(ref, ref, yp_s.at[2 * n + h], yp_r.at[2 * n + h], up_dev)
+
+    def pass_down(yy, h, n):
+        ref = part(core, yy, h)
+        return rcopy(ref, ref, ym_s.at[2 * n + h], ym_r.at[2 * n + h], down_dev)
+
+    def to_sib(core_of, off, h):
+        ref = part(core_of, y + off, h)
+        at = 2 * (off + 4) + h
+        return rcopy(ref, ref, sib_s.at[at], sib_r.at[at], sib_dev)
+
+    sent = []
+
+    def go(c):
         c.start()
-    for n in (1, 2):
-        pass_up(block(y - n), n - 1).wait_recv()
-        nxt = [pass_up(block(y - n), n), to_sib(block(y - n), 2 * n - 1)]
-        for c in nxt:
-            c.start()
-        sent += nxt
-        pass_down(block(y + n), n - 1).wait_recv()
-        nxt = [pass_down(block(y + n), n), to_sib(block(y + n), 2 * n)]
-        for c in nxt:
-            c.start()
-        sent += nxt
-    half = ZX // 2
-    pass_up(block(y - 3), 2).wait_recv()
-    nxt = [pass_up(part(y - 3, 0), 3), to_sib(block(y - 3), 5)]
-    for c in nxt:
-        c.start()
-    sent += nxt
-    pass_down(block(y + 3), 2).wait_recv()
-    nxt = [pass_down(part(y + 3, half), 3), to_sib(block(y + 3), 6)]
-    for c in nxt:
-        c.start()
-    sent += nxt
+        sent.append(c)
+
+    for h in (0, 1):
+        go(pass_up(y, h, 0))
+        go(pass_down(y, h, 0))
+    for h in (0, 1):
+        go(to_sib(core, 0, h))
+    for n in (1, 2, 3):
+        for h in (0, 1):
+            pass_up(y - n, h, n - 1).wait_recv()
+            if n < 3 or h == 0:
+                go(pass_up(y - n, h, n))
+            go(to_sib(core, -n, h))
+            pass_down(y + n, h, n - 1).wait_recv()
+            if n < 3 or h == 1:
+                go(pass_down(y + n, h, n))
+            go(to_sib(core, n, h))
 
     @pl.loop(1, N_REL)
     def _(k):
         p = lax.rem(rel + k, N_REL)
         rcopy(send_buf.at[p], recv.at[p], a_s.at[k], a_r.at[p], {"rel": p}).wait_recv()
 
-    hot_ends[...] = hot(N_REL * SLOTS, ends_row[...])
+    hot_ends[:, pl.ds(0, TRIP)] = hot(N_REL * SLOTS, head_row[...])
+    hot_ends[:, pl.ds(TRIP, TRIP)] = hot(N_REL * SLOTS, tail_row[...])
     ends[...] = select(hot_ends[...], recv[...].reshape(N_REL * SLOTS, WIDTH), TN)
     rel_hot = hot(RELS, rels_row[...])
     ra, rb, rc, rd = quarter(relation[...])
@@ -216,30 +246,15 @@
     dq[...] = pull * tails
     dends[pl.ds(TRIP, TRIP), :] = pull * query[...]
 
-    pass_up(part(y - 4, 0), 3).wait_recv()
-    nxt = [to_sib(part(y - 4, 0), 7)]
-    nxt[0].start()
-    sent += nxt
-    pass_down(part(y + 4, half), 3).wait_recv()
-    nxt = [to_sib(part(y + 4, half), 8)]
-    nxt[0].start()
-    sent += nxt
-
-    def sib_block(yy):
-        return nbuf.at[(1 - core) * NY + lax.rem(yy + 2 * NY, NY)]
-
-    def sib_part(yy, lo):
-        return nbuf.at[(1 - core) * NY + lax.rem(yy + 2 * NY, NY), pl.ds(lo, half)]
-
-    to_sib(sib_block(y), 0).wait_recv()
-    for n in (1, 2, 3):
-        to_sib(sib_block(y - n), 2 * n - 1).wait_recv()
-        to_sib(sib_block(y + n), 2 * n).wait_recv()
-    to_sib(sib_part(y - 4, 0), 7).wait_recv()
-    to_sib(sib_part(y + 4, half), 8).wait_recv()
-
-    @pl.loop(0, 4)
-    def _(b):
+    pass_up(y - 4, 0, 3).wait_recv()
+    go(to_sib(core, -4, 0))
+    pass_down(y + 4, 1, 3).wait_recv()
+    go(to_sib(core, -4, 1))
+    for off in (0, -1, 1, -2, 2, -3, 3, -4):
+        for h in (0, 1):
+            to_sib(1 - core, off, h).wait_recv()
+
+    def score(b):
         q = halves(query[...])
         n = halves(
             jnp.concatenate(
@@ -254,28 +269,20 @@
             gall[b * 4 + w] = dn[:, w * 128 : w * 128 + 128].reshape(ZX, 8, 128)
 
     swap = rcopy(gall.at[pl.ds((1 - core) * NY, NY)], xrecv, x_s, x_r, sib_dev)
-    swap.start()
-    sent.append(swap)
+
+    @pl.loop(0, 2)
+    def _(b):
+        score((1 - core) * 2 + b)
+
+    go(swap)
+
+    @pl.loop(0, 2)
+    def _(b):
+        score(core * 2 + b)
 
     ga, gb, gc, gd = quarter(dq[...])
     ha, hb, hc, hd = quarter(ends[pl.ds(0, TRIP), :])
     ua, ub, uc, ud = quarter(rot[...])
-    dha = ga * ua + gb * ub + gc * uc + gd * ud
-    dhb = gb * ua - ga * ub - gc * ud + gd * uc
-    dhc = gb * ud - ga * uc + gc * ua - gd * ub
-    dhd = gc * ub - ga * ud - gb * uc + gd * ua
-    dends[pl.ds(0, TRIP), :] = jnp.concatenate([dha, dhb, dhc, dhd], axis=1)
-    gt[...] = select(hot_ends[...], dends[...], NN).reshape(N_REL, SLOTS, WIDTH)
-
-    @pl.loop(16, N_REL)
-    def _(k):
-        exchange(gt, ret, b_s, b_r, k)
-
-    @pl.loop(1, 16)
-    def _(k):
-        exchange(gt, ret, b_s, b_r, k)
-
-    ret[rel] = gt[rel]
     dua = ga * ha + gb * hb + gc * hc + gd * hd
     dub = gb * ha - ga * hb + gc * hd - gd * hc
     duc = gc * ha - ga * hc - gb * hd + gd * hb
@@ -300,43 +307,63 @@
     def _(k):
         ring[k, pl.ds(0, ZX)] = gall[core * NY + k] + xrecv[k]
 
-    def chunk(yy, lo, n):
-        return ring.at[lax.rem(yy + 2 * NY, NY), pl.ds(lo, n)]
-
-    def add_up(yy, lo, n, got):
+    def chunk(yy, h):
+        return ring.at[lax.rem(yy + 2 * NY, NY), pl.ds(h * CUT, CUT)]
+
+    def take(yy, h, got, n):
         i = lax.rem(yy + 2 * NY, NY)
-        ring[i, pl.ds(lo, n)] = ring[i, pl.ds(lo, n)] + got[pl.ds(lo, n)]
-
-    def sum_up(yy, lo, n, s):
-        return rcopy(chunk(yy, lo, n), rp.at[s, pl.ds(lo, n)], rp_s.at[s], rp_r.at[s], up_dev)
-
-    def sum_down(yy, lo, n, s):
-        return rcopy(chunk(yy, lo, n), rm.at[s, pl.ds(lo, n)], rm_s.at[s], rm_r.at[s], down_dev)
-
-    nxt = [sum_up(y + 4, 0, 20, 0), sum_down(y - 4, 20, 20, 0)]
-    for c in nxt:
-        c.start()
-    sent += nxt
-    for s in (1, 2, 3):
-        lo_u, n_u, lo_d, n_d = (0, 20, 20, 20) if s == 1 else (0, 40, 0, 40)
-        sum_up(y + 4 - s, lo_u, n_u, s - 1).wait_recv()
-        add_up(y + 4 - s, lo_u, n_u, rp.at[s - 1])
-        c = sum_up(y + 4 - s, 0, 40, s)
-        c.start()
-        sent.append(c)
-        sum_down(y - 4 + s, lo_d, n_d, s - 1).wait_recv()
-        add_up(y - 4 + s, lo_d, n_d, rm.at[s - 1])
-        c = sum_down(y - 4 + s, 0, 40, s)
-        c.start()
-        sent.append(c)
-    sum_up(y, 0, 40, 3).wait_recv()
-    sum_down(y, 0, 40, 3).wait_recv()
+        cols = pl.ds(h * CUT, CUT)
+        ring[i, cols] = ring[i, cols] + got[n, cols]
+
+    def sum_up(yy, h, n):
+        at = 2 * n + h
+        dst = rp.at[n, pl.ds(h * CUT, CUT)]
+        return rcopy(chunk(yy, h), dst, rp_s.at[at], rp_r.at[at], up_dev)
+
+    def sum_down(yy, h, n):
+        at = 2 * n + h
+        dst = rm.at[n, pl.ds(h * CUT, CUT)]
+        return rcopy(chunk(yy, h), dst, rm_s.at[at], rm_r.at[at], down_dev)
+
+    go(sum_up(y + 4, 0, 0))
+    go(sum_down(y - 4, 1, 0))
+    go(sum_up(y + 3, 1, 1))
+    go(sum_down(y - 3, 0, 1))
+
+    dha = ga * ua + gb * ub + gc * uc + gd * ud
+    dhb = gb * ua - ga * ub - gc * ud + gd * uc
+    dhc = gb * ud - ga * uc + gc * ua - gd * ub
+    dhd = gc * ub - ga * ud - gb * uc + gd * ua
+    dends[pl.ds(0, TRIP), :] = jnp.concatenate([dha, dhb, dhc, dhd], axis=1)
+    gt[...] = select(hot_ends[...], dends[...], NN).reshape(N_REL, SLOTS, WIDTH)
+
+    @pl.loop(16, N_REL)
+    def _(k):
+        exchange(gt, ret, b_s, b_r, k)
+
+    @pl.loop(1, 16)
+    def _(k):
+        exchange(gt, ret, b_s, b_r, k)
+
+    ret[rel] = gt[rel]
+
+    for n in (1, 2, 3):
+        for h in (1, 0):
+            if n > 1 or h == 0:
+                sum_up(y + 4 - n, h, n - 1).wait_recv()
+                take(y + 4 - n, h, rp, n - 1)
+                go(sum_up(y + 4 - n, h, n))
+                sum_down(y - 4 + n, 1 - h, n - 1).wait_recv()
+                take(y - 4 + n, 1 - h, rm, n - 1)
+                go(sum_down(y - 4 + n, 1 - h, n))
+    for h in (1, 0):
+        sum_up(y, h, 3).wait_recv()
+        sum_down(y, 1 - h, 3).wait_recv()
     ring[y] = ring[y] + (rp[3] + rm[3])
 
     far = {"dom": (1 - zh) * NY + y}
     cross = rcopy(ring.at[y, pl.ds(ZX, 8)], relx, rx_s, rx_r, far)
-    cross.start()
-    sent.append(cross)
+    go(cross)
 
     @pl.loop(1, ZX)
     def _(k):
@@ -371,7 +398,7 @@
         p = lax.rem(rel + k, N_REL)
         rcopy(gt.at[p], ret.at[p], b_s.at[k], b_r.at[p], {"rel": p}).wait_recv()
 
-    send_hot = hot(ENT, send_row[...])
+    send_hot = hot(ENT, slot_row(send_t))
     grad = select(send_hot, ret[...].reshape(N_REL * SLOTS, WIDTH), NN)
 
     @pl.loop(1, N_DOM)
@@ -386,12 +413,9 @@
         ],
         axis=0,
     )
-    owner = jnp.where(dom == root, 1.0, 0.0).astype(F32)
+    owner = jnp.where(neg_part[...] == dom, 1.0, 0.0).astype(F32)
     neg_hot = hot(ENT, neg_rows[pl.ds(rel, 1), :])
-    grad = grad + owner * select(neg_hot, total, NN)
-    e, ea = adagrad(entity[...], entity_acc[...], grad)
-    new_e[...] = e
-    new_ea[...] = ea
+    grad_e[...] = grad + owner * select(neg_hot, total, NN)
 
     @pl.loop(1, NY)
     def _(k):
@@ -400,13 +424,10 @@
         rcopy(there, there, ra_s.at[k], ra_r.at[i], {"dom": zh * NY + i}).wait_recv()
 
     for w in range(4):
-        cols = pl.ds(w * 128, 128)
         g = jnp.concatenate(
             [rel_full[yy, gg * 4 + w] for yy in range(NY) for gg in range(2)], axis=0
         )
-        r, racc = adagrad(relation[:, cols], relation_acc[:, cols], g)
-        new_r[:, cols] = r
-        new_ra[:, cols] = racc
+        grad_r[:, pl.ds(w * 128, 128)] = g
 
     for c in sent:
         c.wait_send()
@@ -439,19 +460,26 @@
 def shards(
     entity, entity_acc, relation, relation_acc, send_rows, trip_head, trip_rel, trip_tail, neg_part, neg_rows,
 ):
-    send_row = send_rows.reshape(1, N_REL * SLOTS)
-    ends_row = jnp.concatenate([trip_head, trip_tail]).reshape(1, 2 * TRIP)
-    rels_row = trip_rel.reshape(1, TRIP)
+    send_t = send_rows[0].T
+    row = (1, TRIP)
+    anywhere = pl.BlockSpec(memory_space=pl.ANY)
     vmem = pl.BlockSpec(memory_space=pltpu.VMEM)
-    smem = pl.BlockSpec(memory_space=pltpu.SMEM)
     dma = pltpu.SemaphoreType.DMA
     rows = jax.ShapeDtypeStruct((ENT, WIDTH), F32)
-    return pl.pallas_call(
+    grad_e, grad_r = pl.pallas_call(
         kernel,
-        out_shape=(rows, rows, rows, rows),
-        in_specs=[vmem] * 8 + [smem],
-        out_specs=(vmem,) * 4,
+        out_shape=(rows, rows),
+        in_specs=[anywhere] * 8,
+        out_specs=(vmem, vmem),
         scratch_shapes=[
+            pltpu.VMEM((ENT, WIDTH), F32),
+            pltpu.VMEM((RELS, WIDTH), F32),
+            pltpu.VMEM((SLOTS, N_REL), jnp.int32),
+            pltpu.VMEM(row, jnp.int32),
+            pltpu.VMEM(row, jnp.int32),
+            pltpu.VMEM(row, jnp.int32),
+            pltpu.VMEM((N_REL, NEG), jnp.int32),
+            pltpu.VMEM((1, 1), jnp.int32),
             pltpu.VMEM((N_REL, SLOTS, WIDTH), F32),
             pltpu.VMEM((N_REL, SLOTS, WIDTH), F32),
             pltpu.VMEM((N_DOM, *TILE), F32),
@@ -475,11 +503,11 @@
             pltpu.VMEM((NY, 8, *TILE), F32),
             pltpu.VMEM((N_REL, SLOTS, WIDTH), F32),
             pltpu.VMEM((N_REL, SLOTS, WIDTH), F32),
-            dma((N_REL,)), dma((N_REL,)), dma((N_REL,)), dma((N_REL,)),
+            dma((8,)), dma((N_REL,)), dma((N_REL,)), dma((N_REL,)), dma((N_REL,)),
             dma((N_DOM,)), dma((N_DOM,)), dma((ZX,)), dma((ZX,)),
-            dma((4,)), dma((4,)), dma((4,)), dma((4,)),
-            dma((9,)), dma((9,)), dma, dma,
-            dma((4,)), dma((4,)), dma((4,)), dma((4,)),
+            dma((8,)), dma((8,)), dma((8,)), dma((8,)),
+            dma((16,)), dma((16,)), dma, dma,
+            dma((8,)), dma((8,)), dma((8,)), dma((8,)),
             dma((ZX,)), dma((ZX,)), dma, dma,
             dma((N_DOM,)), dma((N_DOM,)), dma((NY,)), dma((NY,)),
         ],
@@ -487,7 +515,14 @@
             collective_id=0, has_side_effects=True, vmem_limit_bytes=56 << 20
         ),
         name="step",
-    )(entity, entity_acc, relation, relation_acc, send_row, ends_row, rels_row, neg_rows, neg_part)
+    )(
+        entity, relation, send_t, trip_head.reshape(row), trip_tail.reshape(row),
+        trip_rel.reshape(row), neg_rows, neg_part.reshape(1, 1),
+    )
+    return (
+        *adagrad(entity, entity_acc, grad_e),
+        *adagrad(relation, relation_acc, grad_r),
+    )
 
 
 def solution(mesh):

time: 125 us -> 114 us (0.912)
  Pallas kernels: 117 us -> 109 us
  local copies, waits for them, and re-layouts: 5.25 us -> 0.01 us
    pallas_call x1, Pallas kernels: 117 us -> 109 us  [shards(): pl.pallas_call(kernel, out_shape=(rows, rows), in_specs=[anywhere] * 8, o...]
    unnamed x13 -> x4, local copies, waits for them, and re-layouts: 4.58 us -> 0.01 us
    sub x0 -> x1, other arithmetic: none -> 2.22 us  [adagrad(): return (values - step_size * gradient / jnp.sqrt(history_new), history_new)]
    concatenate x1 -> x0, other arithmetic: 1.28 us -> none  [shards(): ends_row = jnp.concatenate([trip_head, trip_tail]).reshape(1, 2 * TRIP)]
where the time goes in v2:
time: 114 us; the launch traced here: 113 us
  Pallas kernels  109 us (96%)
  other arithmetic  2.22 us (2%)
  between operations  1.32 us (1%)
    pallas_call x1, Pallas kernels, shards(): pl.pallas_call(kernel, out_shape=(rows, rows), in_specs=[anywhere] * 8, o...  109 us

profile of v2, /device:TPU:1, one launch (start us, length us, event | category | flops | bytes accessed | tf_op | source)
XLA Modules:
  0.0 112.9 jit_solution(13536905965384308311)
XLA Ops:
  1.3 0.0 copy-start
  1.3 0.0 copy-start.1
  1.3 109.3 %step.1 = (f32[128,512]{1,0:T(8,128)}, f32[128,512]{1,0:T(8,128)}) custom-call(f32[128,512]{1,0:T(8,128)} %entity_h.1, f32[128,512]{1,0:T(8,128)} %relation_h.1, s32[16,32]{1,0:T(8,128)} %bitcast.8, s32[1,256]{1,0:T(1,128)} %bitcast.9, s32[1,256]{1,0:T(1,128)} %bitcast.10, s32[1,256]{1,0:T(1,128)} %bitcast.11, s32[32,32]{1,0:T(8,128)} %neg_h.1, ...), custom_call_target="tpu_custom_call" | custom-call | tf_op jit(solution)/shard_map/step/pallas_call | solution.py:469
  110.6 0.0 copy-done
  110.7 0.0 copy-done.1
  110.7 2.2 %multiply_subtract_fusion = (f32[128,512]{1,0:T(8,128)}, f32[128,512]{1,0:T(8,128)}, f32[128,512]{1,0:T(8,128)}, f32[128,512]{1,0:T(8,128)}) fusion(f32[128,512]{1,0:T(8,128)S(1)} %copy-done, f32[128,512]{1,0:T(8,128)} %get-tuple-element.7, f32[128,512]{1,0:T(8,128)} %param.13, f32[128,512]{1,0:T(8,128)S(1)} %copy-done.1, f32[128,512]{1,0:T(8,128)} %param.11, ...), kind=kLoop, calls=%fused_computation | loop fusion | flops 655360 | bytes 2621440 | tf_op jit(solution)/shard_map/sub | solution.py:75
Async XLA Ops:
  1.3 109.4 %copy-start = (f32[128,512]{1,0:T(8,128)S(1)}, f32[128,512]{1,0:T(8,128)}, u32[]{:S(2)}) copy-start(f32[128,512]{1,0:T(8,128)} %relation_h.1) | copy-start | bytes 786436
  1.3 109.4 %copy-start.1 = (f32[128,512]{1,0:T(8,128)S(1)}, f32[128,512]{1,0:T(8,128)}, u32[]{:S(2)}) copy-start(f32[128,512]{1,0:T(8,128)} %entity_h.1) | copy-start | bytes 786436

commit v3 on v2

--- a/solution.py
+++ b/solution.py
@@ -15,7 +15,8 @@
 ENT, RELS, TRIP, SLOTS, NEG, WIDTH = 128, 128, 256, 16, 32, 512
 TILE = (8, 128)
 NEGS = NEG * N_REL
-FIRST = 24
+AHEAD = (8, 12, 15, 18, 21, 24, 27, 32)
+BACK = (9, 12, 14, 16, 18, 20, 32)
 HALF = ZX // 2
 CUT = 20
 
@@ -147,13 +148,25 @@
         p = lax.rem(dom + k, N_DOM)
         rcopy(neg_src.at[p], s1_recv.at[dom], s1_s.at[k], s1_r.at[dom], {"dom": p}).start()
 
-    def exchange(src, dst, ssem, rsem, k):
-        p = lax.rem(rel + k, N_REL)
-        rcopy(src.at[p], dst.at[rel], ssem.at[k], rsem.at[rel], {"rel": p}).start()
-
-    @pl.loop(FIRST, N_REL)
-    def _(k):
-        exchange(send_buf, recv, a_s, a_r, k)
+    def peer(k):
+        pz = lax.rem(lax.div(rel, 8) + lax.rem(k, 4), 4)
+        px = lax.rem(lax.div(lax.rem(rel, 8), 2) + lax.div(k, 8), NX)
+        pc = lax.rem(core + lax.rem(lax.div(k, 4), 2), 2)
+        return pz * 8 + px * 2 + pc
+
+    def exchange(src, dst, ssem, rsem, lo, hi):
+        @pl.loop(lo, hi)
+        def _(k):
+            p = peer(k)
+            rcopy(src.at[p], dst.at[rel], ssem.at[k], rsem.at[rel], {"rel": p}).start()
+
+    def ahead(n):
+        exchange(send_buf, recv, a_s, a_r, AHEAD[n - 1] if n else 1, AHEAD[n])
+
+    def back(n):
+        exchange(gt, ret, b_s, b_r, BACK[n - 1] if n else 1, BACK[n])
+
+    ahead(0)
 
     s1_recv[dom] = neg_src[dom]
     recv[rel] = send_buf[rel]
@@ -172,9 +185,7 @@
         here = nbuf.at[mine, zi]
         rcopy(here, here, s2_s.at[k], s2_r.at[zi], zx_dev(p)).start()
 
-    @pl.loop(1, FIRST)
-    def _(k):
-        exchange(send_buf, recv, a_s, a_r, k)
+    ahead(1)
 
     @pl.loop(1, ZX)
     def _(k):
@@ -219,6 +230,7 @@
             if n < 3 or h == 1:
                 go(pass_down(y + n, h, n))
             go(to_sib(core, n, h))
+            ahead(2 * n + h)
 
     @pl.loop(1, N_REL)
     def _(k):
@@ -337,15 +349,8 @@
     dends[pl.ds(0, TRIP), :] = jnp.concatenate([dha, dhb, dhc, dhd], axis=1)
     gt[...] = select(hot_ends[...], dends[...], NN).reshape(N_REL, SLOTS, WIDTH)
 
-    @pl.loop(16, N_REL)
-    def _(k):
-        exchange(gt, ret, b_s, b_r, k)
-
-    @pl.loop(1, 16)
-    def _(k):
-        exchange(gt, ret, b_s, b_r, k)
-
     ret[rel] = gt[rel]
+    back(0)
 
     for n in (1, 2, 3):
         for h in (1, 0):
@@ -356,6 +361,7 @@
                 sum_down(y - 4 + n, 1 - h, n - 1).wait_recv()
                 take(y - 4 + n, 1 - h, rm, n - 1)
                 go(sum_down(y - 4 + n, 1 - h, n))
+                back(2 * n - 1 - h)
     for h in (1, 0):
         sum_up(y, h, 3).wait_recv()
         sum_down(y, 1 - h, 3).wait_recv()
@@ -370,6 +376,7 @@
         p = lax.rem(zi + k, ZX)
         rcopy(ring.at[y, p], zx_recv.at[zi], z_s.at[k], z_r.at[zi], zx_dev(p)).start()
 
+    back(6)
     zx_recv[zi] = ring[y, zi]
 
     @pl.loop(1, ZX)

time: 114 us -> 101 us (0.89)
  Pallas kernels: 109 us -> 96.2 us
    pallas_call x1, Pallas kernels: 109 us -> 96.2 us  [shards(): pl.pallas_call(kernel, out_shape=(rows, rows), in_specs=[anywhere] * 8, o...]
where the time goes in v3:
time: 101 us; the launch traced here: 99.7 us
  Pallas kernels  96.2 us (95%)
  other arithmetic  2.22 us (2%)
  between operations  1.32 us (1%)
    pallas_call x1, Pallas kernels, shards(): pl.pallas_call(kernel, out_shape=(rows, rows), in_specs=[anywhere] * 8, o...  96.2 us
    sub x1, other arithmetic, adagrad(): return (values - step_size * gradient / jnp.sqrt(history_new), history_new)  2.22 us

profile of v3, /device:TPU:1, one launch (start us, length us, event | category | flops | bytes accessed | tf_op | source)
XLA Modules:
  0.0 99.7 jit_solution(9713872738304149965)
XLA Ops:
  1.3 0.0 copy-start
  1.3 0.0 copy-start.1
  1.3 96.2 %step.1 = (f32[128,512]{1,0:T(8,128)}, f32[128,512]{1,0:T(8,128)}) custom-call(f32[128,512]{1,0:T(8,128)} %entity_h.1, f32[128,512]{1,0:T(8,128)} %relation_h.1, s32[16,32]{1,0:T(8,128)} %bitcast.8, s32[1,256]{1,0:T(1,128)} %bitcast.9, s32[1,256]{1,0:T(1,128)} %bitcast.10, s32[1,256]{1,0:T(1,128)} %bitcast.11, s32[32,32]{1,0:T(8,128)} %neg_h.1, ...), custom_call_target="tpu_custom_call" | custom-call | tf_op jit(solution)/shard_map/step/pallas_call | solution.py:476
  97.5 0.0 copy-done
  97.5 0.0 copy-done.1
  97.5 2.2 %multiply_subtract_fusion = (f32[128,512]{1,0:T(8,128)}, f32[128,512]{1,0:T(8,128)}, f32[128,512]{1,0:T(8,128)}, f32[128,512]{1,0:T(8,128)}) fusion(f32[128,512]{1,0:T(8,128)S(1)} %copy-done, f32[128,512]{1,0:T(8,128)} %get-tuple-element.7, f32[128,512]{1,0:T(8,128)} %param.13, f32[128,512]{1,0:T(8,128)S(1)} %copy-done.1, f32[128,512]{1,0:T(8,128)} %param.11, ...), kind=kLoop, calls=%fused_computation | loop fusion | flops 655360 | bytes 2621440 | tf_op jit(solution)/shard_map/sub | solution.py:76
Async XLA Ops:
  1.3 96.2 %copy-start = (f32[128,512]{1,0:T(8,128)S(1)}, f32[128,512]{1,0:T(8,128)}, u32[]{:S(2)}) copy-start(f32[128,512]{1,0:T(8,128)} %relation_h.1) | copy-start | bytes 786436
  1.3 96.2 %copy-start.1 = (f32[128,512]{1,0:T(8,128)S(1)}, f32[128,512]{1,0:T(8,128)}, u32[]{:S(2)}) copy-start(f32[128,512]{1,0:T(8,128)} %entity_h.1) | copy-start | bytes 786436

commit v4 on v3

--- a/solution.py
+++ b/solution.py
@@ -15,7 +15,7 @@
 ENT, RELS, TRIP, SLOTS, NEG, WIDTH = 128, 128, 256, 16, 32, 512
 TILE = (8, 128)
 NEGS = NEG * N_REL
-AHEAD = (8, 12, 15, 18, 21, 24, 27, 32)
+AHEAD = (11, 18, 20, 22, 24, 26, 28, 32)
 BACK = (9, 12, 14, 16, 18, 20, 32)
 HALF = ZX // 2
 CUT = 20
@@ -81,6 +81,7 @@
     grad_e, grad_r,
     entity, relation, send_t, head_row, tail_row, rels_row, neg_rows, neg_part,
     send_buf, recv, neg_src, s1_recv, nbuf, hot_ends, ends, rot, query, dq, dends,
+    rel_hot, unit, scale, q_hi, q_lo,
     gall, xrecv, ring, rp, rm, zx_recv, relx, tile_out, t_recv, rel_full, gt, ret,
     in_s, a_s, a_r, b_s, b_r, s1_s, s1_r, s2_s, s2_r, yp_s, yp_r, ym_s, ym_r, sib_s, sib_r, x_s, x_r,
     rp_s, rp_r, rm_s, rm_r, z_s, z_r, rx_s, rx_r, t_s, t_r, ra_s, ra_r,
@@ -107,12 +108,22 @@
     def zx_dev(p):
         return {"dom": lax.div(p, 16) * NY + y, "rel": lax.rem(p, 16) * 2 + core}
 
+    def fan(j, n):
+        return n // 2 + lax.div(j + 1, 2) * (1 - 2 * lax.rem(j, 2))
+
+    def zx_peer(j):
+        return lax.rem(zi + fan(j, ZX), ZX)
+
+    def dom_peer(j):
+        other = lax.rem(zh + 1 - lax.div(j, NY), 2)
+        return other * NY + lax.rem(y + fan(lax.rem(j, NY), NY), NY)
+
     barrier = pltpu.get_barrier_semaphore()
 
-    @pl.loop(1, N_DOM)
+    @pl.loop(0, N_DOM - 1)
     def _(k):
         pl.semaphore_signal(
-            barrier, inc=1, device_id={"dom": lax.rem(dom + k, N_DOM)}, device_id_type=MESH
+            barrier, inc=1, device_id={"dom": dom_peer(k)}, device_id_type=MESH
         )
 
     @pl.loop(1, N_REL)
@@ -143,9 +154,9 @@
 
     pl.semaphore_wait(barrier, (N_DOM - 1) + (N_REL - 1) + 15)
 
-    @pl.loop(1, N_DOM)
-    def _(k):
-        p = lax.rem(dom + k, N_DOM)
+    @pl.loop(0, N_DOM - 1)
+    def _(k):
+        p = dom_peer(k)
         rcopy(neg_src.at[p], s1_recv.at[dom], s1_s.at[k], s1_r.at[dom], {"dom": p}).start()
 
     def peer(k):
@@ -171,25 +182,25 @@
     s1_recv[dom] = neg_src[dom]
     recv[rel] = send_buf[rel]
 
-    @pl.loop(1, N_DOM)
-    def _(k):
-        p = lax.rem(dom + k, N_DOM)
+    @pl.loop(0, N_DOM - 1)
+    def _(k):
+        p = dom_peer(k)
         rcopy(neg_src.at[p], s1_recv.at[p], s1_s.at[k], s1_r.at[p], {"dom": p}).wait_recv()
 
     mine = core * NY + y
     nbuf[mine, zi] = jnp.sum(jnp.where(is_root, s1_recv[...], 0.0), axis=0)
 
-    @pl.loop(1, ZX)
-    def _(k):
-        p = lax.rem(zi + k, ZX)
+    @pl.loop(0, ZX - 1)
+    def _(k):
+        p = zx_peer(k)
         here = nbuf.at[mine, zi]
         rcopy(here, here, s2_s.at[k], s2_r.at[zi], zx_dev(p)).start()
 
     ahead(1)
 
-    @pl.loop(1, ZX)
-    def _(k):
-        p = lax.rem(zi + k, ZX)
+    @pl.loop(0, ZX - 1)
+    def _(k):
+        p = zx_peer(k)
         there = nbuf.at[mine, p]
         rcopy(there, there, s2_s.at[k], s2_r.at[p], zx_dev(p)).wait_recv()
 
@@ -232,19 +243,21 @@
             go(to_sib(core, n, h))
             ahead(2 * n + h)
 
+    rel_hot[...] = hot(RELS, rels_row[...])
+    ra, rb, rc, rd = quarter(relation[...])
+    inv = 1.0 / jnp.sqrt(ra * ra + rb * rb + rc * rc + rd * rd)
+    scale[...] = inv
+    unit[...] = jnp.concatenate([ra * inv, rb * inv, rc * inv, rd * inv], axis=1)
+    rot[...] = select(rel_hot[...], unit[...], TN)
+    hot_ends[:, pl.ds(0, TRIP)] = hot(N_REL * SLOTS, head_row[...])
+    hot_ends[:, pl.ds(TRIP, TRIP)] = hot(N_REL * SLOTS, tail_row[...])
+
     @pl.loop(1, N_REL)
     def _(k):
         p = lax.rem(rel + k, N_REL)
         rcopy(send_buf.at[p], recv.at[p], a_s.at[k], a_r.at[p], {"rel": p}).wait_recv()
 
-    hot_ends[:, pl.ds(0, TRIP)] = hot(N_REL * SLOTS, head_row[...])
-    hot_ends[:, pl.ds(TRIP, TRIP)] = hot(N_REL * SLOTS, tail_row[...])
     ends[...] = select(hot_ends[...], recv[...].reshape(N_REL * SLOTS, WIDTH), TN)
-    rel_hot = hot(RELS, rels_row[...])
-    ra, rb, rc, rd = quarter(relation[...])
-    inv = 1.0 / jnp.sqrt(ra * ra + rb * rb + rc * rc + rd * rd)
-    unit = jnp.concatenate([ra * inv, rb * inv, rc * inv, rd * inv], axis=1)
-    rot[...] = select(rel_hot, unit, TN)
     ha, hb, hc, hd = quarter(ends[pl.ds(0, TRIP), :])
     ua, ub, uc, ud = quarter(rot[...])
     qa = ha * ua - hb * ub - hc * uc - hd * ud
@@ -252,6 +265,7 @@
     qc = ha * uc - hb * ud + hc * ua + hd * ub
     qd = ha * ud + hb * uc - hc * ub + hd * ua
     query[...] = jnp.concatenate([qa, qb, qc, qd], axis=1)
+    q_hi[...], q_lo[...] = halves(query[...])
     tails = ends[pl.ds(TRIP, TRIP), :]
     positive = jnp.sum(query[...] * tails, axis=1, keepdims=True)
     pull = -1.0 / (1.0 + jnp.exp(positive))
@@ -262,12 +276,8 @@
     go(to_sib(core, -4, 0))
     pass_down(y + 4, 1, 3).wait_recv()
     go(to_sib(core, -4, 1))
-    for off in (0, -1, 1, -2, 2, -3, 3, -4):
-        for h in (0, 1):
-            to_sib(1 - core, off, h).wait_recv()
-
     def score(b):
-        q = halves(query[...])
+        q = q_hi[...], q_lo[...]
         n = halves(
             jnp.concatenate(
                 [nbuf[b * 4 + w].reshape(ZX * 8, 128) for w in range(4)], axis=1
@@ -280,30 +290,39 @@
         for w in range(4):
             gall[b * 4 + w] = dn[:, w * 128 : w * 128 + 128].reshape(ZX, 8, 128)
 
-    swap = rcopy(gall.at[pl.ds((1 - core) * NY, NY)], xrecv, x_s, x_r, sib_dev)
-
-    @pl.loop(0, 2)
-    def _(b):
-        score((1 - core) * 2 + b)
-
-    go(swap)
-
-    @pl.loop(0, 2)
-    def _(b):
-        score(core * 2 + b)
+    def swap(of, h):
+        src = gall.at[pl.ds(of * NY + 4 * h, 4)]
+        return rcopy(src, xrecv.at[pl.ds(4 * h, 4)], x_s.at[h], x_r.at[h], sib_dev)
+
+    score(core * 2)
+    for off in (0, -1, 1, -2, 2, -3, 3, -4):
+        for h in (0, 1):
+            to_sib(1 - core, off, h).wait_recv()
+    score((1 - core) * 2)
+    go(swap(1 - core, 0))
+    score((1 - core) * 2 + 1)
+    go(swap(1 - core, 1))
+    score(core * 2 + 1)
 
     ga, gb, gc, gd = quarter(dq[...])
     ha, hb, hc, hd = quarter(ends[pl.ds(0, TRIP), :])
     ua, ub, uc, ud = quarter(rot[...])
+    dha = ga * ua + gb * ub + gc * uc + gd * ud
+    dhb = gb * ua - ga * ub - gc * ud + gd * uc
+    dhc = gb * ud - ga * uc + gc * ua - gd * ub
+    dhd = gc * ub - ga * ud - gb * uc + gd * ua
+    dends[pl.ds(0, TRIP), :] = jnp.concatenate([dha, dhb, dhc, dhd], axis=1)
+    gt[...] = select(hot_ends[...], dends[...], NN).reshape(N_REL, SLOTS, WIDTH)
+
+    ret[rel] = gt[rel]
+    back(0)
     dua = ga * ha + gb * hb + gc * hc + gd * hd
     dub = gb * ha - ga * hb + gc * hd - gd * hc
     duc = gc * ha - ga * hc - gb * hd + gd * hb
     dud = gb * hc - ga * hd - gc * hb + gd * ha
-    rel_hot = hot(RELS, rels_row[...])
-    du = select(rel_hot, jnp.concatenate([dua, dub, duc, dud], axis=1), NN)
-    ra, rb, rc, rd = quarter(relation[...])
-    inv = 1.0 / jnp.sqrt(ra * ra + rb * rb + rc * rc + rd * rd)
-    va, vb, vc, vd = ra * inv, rb * inv, rc * inv, rd * inv
+    du = select(rel_hot[...], jnp.concatenate([dua, dub, duc, dud], axis=1), NN)
+    va, vb, vc, vd = quarter(unit[...])
+    inv = scale[...]
     da, db, dc, dd = quarter(du)
     along = da * va + db * vb + dc * vc + dd * vd
     parts = [(g - v * along) * inv for g, v in ((da, va), (db, vb), (dc, vc), (dd, vd))]
@@ -313,7 +332,8 @@
                 at = yy * 16 + g * 8
                 ring[yy, ZX + g * 4 + w] = parts[w][at : at + 8, :]
 
-    rcopy(gall.at[pl.ds(core * NY, NY)], xrecv, x_s, x_r, sib_dev).wait_recv()
+    for h in (0, 1):
+        swap(core, h).wait_recv()
 
     @pl.loop(0, NY)
     def _(k):
@@ -341,16 +361,6 @@
     go(sum_down(y - 4, 1, 0))
     go(sum_up(y + 3, 1, 1))
     go(sum_down(y - 3, 0, 1))
-
-    dha = ga * ua + gb * ub + gc * uc + gd * ud
-    dhb = gb * ua - ga * ub - gc * ud + gd * uc
-    dhc = gb * ud - ga * uc + gc * ua - gd * ub
-    dhd = gc * ub - ga * ud - gb * uc + gd * ua
-    dends[pl.ds(0, TRIP), :] = jnp.concatenate([dha, dhb, dhc, dhd], axis=1)
-    gt[...] = select(hot_ends[...], dends[...], NN).reshape(N_REL, SLOTS, WIDTH)
-
-    ret[rel] = gt[rel]
-    back(0)
 
     for n in (1, 2, 3):
         for h in (1, 0):
@@ -371,24 +381,24 @@
     cross = rcopy(ring.at[y, pl.ds(ZX, 8)], relx, rx_s, rx_r, far)
     go(cross)
 
-    @pl.loop(1, ZX)
-    def _(k):
-        p = lax.rem(zi + k, ZX)
+    @pl.loop(0, ZX - 1)
+    def _(k):
+        p = zx_peer(k)
         rcopy(ring.at[y, p], zx_recv.at[zi], z_s.at[k], z_r.at[zi], zx_dev(p)).start()
 
     back(6)
     zx_recv[zi] = ring[y, zi]
 
-    @pl.loop(1, ZX)
-    def _(k):
-        p = lax.rem(zi + k, ZX)
+    @pl.loop(0, ZX - 1)
+    def _(k):
+        p = zx_peer(k)
         rcopy(ring.at[y, p], zx_recv.at[p], z_s.at[k], z_r.at[p], zx_dev(p)).wait_recv()
 
     tile_out[...] = jnp.sum(zx_recv[...], axis=0)
 
-    @pl.loop(1, N_DOM)
-    def _(k):
-        p = lax.rem(dom + k, N_DOM)
+    @pl.loop(0, N_DOM - 1)
+    def _(k):
+        p = dom_peer(k)
         rcopy(tile_out, t_recv.at[dom], t_s.at[k], t_r.at[dom], {"dom": p}).start()
 
     t_recv[dom] = tile_out[...]
@@ -408,9 +418,9 @@
     send_hot = hot(ENT, slot_row(send_t))
     grad = select(send_hot, ret[...].reshape(N_REL * SLOTS, WIDTH), NN)
 
-    @pl.loop(1, N_DOM)
-    def _(k):
-        p = lax.rem(dom + k, N_DOM)
+    @pl.loop(0, N_DOM - 1)
+    def _(k):
+        p = dom_peer(k)
         rcopy(tile_out, t_recv.at[p], t_s.at[k], t_r.at[p], {"dom": p}).wait_recv()
 
     total = jnp.concatenate(
@@ -439,9 +449,9 @@
     for c in sent:
         c.wait_send()
 
-    @pl.loop(1, N_DOM)
-    def _(k):
-        p = lax.rem(dom + k, N_DOM)
+    @pl.loop(0, N_DOM - 1)
+    def _(k):
+        p = dom_peer(k)
         rcopy(neg_src.at[p], s1_recv.at[dom], s1_s.at[k], s1_r.at[dom], {"dom": p}).wait_send()
         rcopy(tile_out, t_recv.at[dom], t_s.at[k], t_r.at[dom], {"dom": p}).wait_send()
 
@@ -451,9 +461,9 @@
         rcopy(send_buf.at[p], recv.at[rel], a_s.at[k], a_r.at[rel], {"rel": p}).wait_send()
         rcopy(gt.at[p], ret.at[rel], b_s.at[k], b_r.at[rel], {"rel": p}).wait_send()
 
-    @pl.loop(1, ZX)
-    def _(k):
-        p = lax.rem(zi + k, ZX)
+    @pl.loop(0, ZX - 1)
+    def _(k):
+        p = zx_peer(k)
         here = nbuf.at[mine, zi]
         rcopy(here, here, s2_s.at[k], s2_r.at[zi], zx_dev(p)).wait_send()
         rcopy(ring.at[y, p], zx_recv.at[zi], z_s.at[k], z_r.at[zi], zx_dev(p)).wait_send()
@@ -498,6 +508,11 @@
             pltpu.VMEM((TRIP, WIDTH), F32),
             pltpu.VMEM((TRIP, WIDTH), F32),
             pltpu.VMEM((2 * TRIP, WIDTH), F32),
+            pltpu.VMEM((RELS, TRIP), BF16),
+            pltpu.VMEM((RELS, WIDTH), F32),
+            pltpu.VMEM((RELS, WIDTH // 4), F32),
+            pltpu.VMEM((TRIP, WIDTH), BF16),
+            pltpu.VMEM((TRIP, WIDTH), BF16),
             pltpu.VMEM((2 * NY, ZX, *TILE), F32),
             pltpu.VMEM((NY, ZX, *TILE), F32),
             pltpu.VMEM((NY, ZX + 8, *TILE), F32),
@@ -513,7 +528,7 @@
             dma((8,)), dma((N_REL,)), dma((N_REL,)), dma((N_REL,)), dma((N_REL,)),
             dma((N_DOM,)), dma((N_DOM,)), dma((ZX,)), dma((ZX,)),
             dma((8,)), dma((8,)), dma((8,)), dma((8,)),
-            dma((16,)), dma((16,)), dma, dma,
+            dma((16,)), dma((16,)), dma((2,)), dma((2,)),
             dma((8,)), dma((8,)), dma((8,)), dma((8,)),
             dma((ZX,)), dma((ZX,)), dma, dma,
             dma((N_DOM,)), dma((N_DOM,)), dma((NY,)), dma((NY,)),

time: 101 us -> 100 us (0.990)
  no operation moved by 1% of the time
where the time goes in v4:
time: 100 us; the launch traced here: 99.7 us
  Pallas kernels  96.1 us (96%)
  other arithmetic  2.22 us (2%)
  between operations  1.32 us (1%)
    pallas_call x1, Pallas kernels, shards(): pl.pallas_call(kernel, out_shape=(rows, rows), in_specs=[anywhere] * 8, o...  96.1 us
    sub x1, other arithmetic, adagrad(): return (values - step_size * gradient / jnp.sqrt(history_new), history_new)  2.22 us

profile of v4, /device:TPU:1, one launch (start us, length us, event | category | flops | bytes accessed | tf_op | source)
XLA Modules:
  0.0 99.7 jit_solution(15305763132122014399)
XLA Ops:
  1.3 0.0 copy-start
  1.3 0.0 copy-start.1
  1.3 96.1 %step.1 = (f32[128,512]{1,0:T(8,128)}, f32[128,512]{1,0:T(8,128)}) custom-call(f32[128,512]{1,0:T(8,128)} %entity_h.1, f32[128,512]{1,0:T(8,128)} %relation_h.1, s32[16,32]{1,0:T(8,128)} %bitcast.8, s32[1,256]{1,0:T(1,128)} %bitcast.9, s32[1,256]{1,0:T(1,128)} %bitcast.10, s32[1,256]{1,0:T(1,128)} %bitcast.11, s32[32,32]{1,0:T(8,128)} %neg_h.1, ...), custom_call_target="tpu_custom_call" | custom-call | tf_op jit(solution)/shard_map/step/pallas_call | solution.py:486
  97.4 0.0 copy-done
  97.4 0.0 copy-done.1
  97.5 2.2 %multiply_subtract_fusion = (f32[128,512]{1,0:T(8,128)}, f32[128,512]{1,0:T(8,128)}, f32[128,512]{1,0:T(8,128)}, f32[128,512]{1,0:T(8,128)}) fusion(f32[128,512]{1,0:T(8,128)S(1)} %copy-done, f32[128,512]{1,0:T(8,128)} %get-tuple-element.7, f32[128,512]{1,0:T(8,128)} %param.13, f32[128,512]{1,0:T(8,128)S(1)} %copy-done.1, f32[128,512]{1,0:T(8,128)} %param.11, ...), kind=kLoop, calls=%fused_computation | loop fusion | flops 655360 | bytes 2621440 | tf_op jit(solution)/shard_map/sub | solution.py:76
Async XLA Ops:
  1.3 96.2 %copy-start = (f32[128,512]{1,0:T(8,128)S(1)}, f32[128,512]{1,0:T(8,128)}, u32[]{:S(2)}) copy-start(f32[128,512]{1,0:T(8,128)} %relation_h.1) | copy-start | bytes 786436
  1.3 96.2 %copy-start.1 = (f32[128,512]{1,0:T(8,128)S(1)}, f32[128,512]{1,0:T(8,128)}, u32[]{:S(2)}) copy-start(f32[128,512]{1,0:T(8,128)} %entity_h.1) | copy-start | bytes 786436

commit v5 on v4

--- a/solution.py
+++ b/solution.py
@@ -15,10 +15,9 @@
 ENT, RELS, TRIP, SLOTS, NEG, WIDTH = 128, 128, 256, 16, 32, 512
 TILE = (8, 128)
 NEGS = NEG * N_REL
-AHEAD = (11, 18, 20, 22, 24, 26, 28, 32)
+AHEAD = (8, 12, 15, 18, 21, 24, 27, 32)
 BACK = (9, 12, 14, 16, 18, 20, 32)
 HALF = ZX // 2
-CUT = 20
 
 NN = (((1,), (0,)), ((), ()))
 TN = (((0,), (0,)), ((), ()))
@@ -81,10 +80,11 @@
     grad_e, grad_r,
     entity, relation, send_t, head_row, tail_row, rels_row, neg_rows, neg_part,
     send_buf, recv, neg_src, s1_recv, nbuf, hot_ends, ends, rot, query, dq, dends,
-    rel_hot, unit, scale, q_hi, q_lo,
+    rel_hot, unit, scale, q_hi, q_lo, rring, rrp, rrm,
     gall, xrecv, ring, rp, rm, zx_recv, relx, tile_out, t_recv, rel_full, gt, ret,
     in_s, a_s, a_r, b_s, b_r, s1_s, s1_r, s2_s, s2_r, yp_s, yp_r, ym_s, ym_r, sib_s, sib_r, x_s, x_r,
     rp_s, rp_r, rm_s, rm_r, z_s, z_r, rx_s, rx_r, t_s, t_r, ra_s, ra_r,
+    up_s, up_r, dn_s, dn_r,
 ):
     loads = [
         pltpu.make_async_copy(h, v, in_s.at[n])
@@ -294,15 +294,77 @@
         src = gall.at[pl.ds(of * NY + 4 * h, 4)]
         return rcopy(src, xrecv.at[pl.ds(4 * h, 4)], x_s.at[h], x_r.at[h], sib_dev)
 
-    score(core * 2)
+    def chunk(yy, h):
+        return ring.at[lax.rem(yy + 2 * NY, NY), pl.ds(h * HALF, HALF)]
+
+    def take(yy, h, got, n):
+        i = lax.rem(yy + 2 * NY, NY)
+        cols = pl.ds(h * HALF, HALF)
+        ring[i, cols] = ring[i, cols] + got[n, cols]
+
+    def sum_up(yy, h, n):
+        at = 2 * n + h
+        dst = rp.at[n, pl.ds(h * HALF, HALF)]
+        return rcopy(chunk(yy, h), dst, rp_s.at[at], rp_r.at[at], up_dev)
+
+    def sum_down(yy, h, n):
+        at = 2 * n + h
+        dst = rm.at[n, pl.ds(h * HALF, HALF)]
+        return rcopy(chunk(yy, h), dst, rm_s.at[at], rm_r.at[at], down_dev)
+
+    def neg_step(n, h):
+        sum_up(y + 4 - n, h, n - 1).wait_recv()
+        take(y + 4 - n, h, rp, n - 1)
+        go(sum_up(y + 4 - n, h, n))
+        sum_down(y - 4 + n, 1 - h, n - 1).wait_recv()
+        take(y - 4 + n, 1 - h, rm, n - 1)
+        go(sum_down(y - 4 + n, 1 - h, n))
+
+    def rel_up(n):
+        cols = pl.ds(0, 8 if n else 4)
+        src = rring.at[lax.rem(y + 4 - n, NY), cols]
+        return rcopy(src, rrp.at[n, cols], up_s.at[n], up_r.at[n], up_dev)
+
+    def rel_down(n):
+        cols = pl.ds(0, 8) if n else pl.ds(4, 4)
+        src = rring.at[lax.rem(y + 4 + n, NY), cols]
+        return rcopy(src, rrm.at[n, cols], dn_s.at[n], dn_r.at[n], down_dev)
+
+    def rel_step(n):
+        u, d = lax.rem(y + 4 - n, NY), lax.rem(y + 4 + n, NY)
+        uc, dc = (pl.ds(0, 4), pl.ds(4, 4)) if n == 1 else (pl.ds(0, 8), pl.ds(0, 8))
+        rel_up(n - 1).wait_recv()
+        rring[u, uc] = rring[u, uc] + rrp[n - 1, uc]
+        go(rel_up(n))
+        rel_down(n - 1).wait_recv()
+        rring[d, dc] = rring[d, dc] + rrm[n - 1, dc]
+        go(rel_down(n))
+
+    def merge(h):
+        swap(core, h).wait_recv()
+
+        @pl.loop(0, 4)
+        def _(k):
+            i = h * 4 + k
+            ring[i] = gall[core * NY + i] + xrecv[i]
+
+    near = lax.div(y, 4)
+    away = 1 - near
+    score(core * 2 + away)
     for off in (0, -1, 1, -2, 2, -3, 3, -4):
         for h in (0, 1):
             to_sib(1 - core, off, h).wait_recv()
-    score((1 - core) * 2)
-    go(swap(1 - core, 0))
-    score((1 - core) * 2 + 1)
-    go(swap(1 - core, 1))
-    score(core * 2 + 1)
+    score((1 - core) * 2 + away)
+    go(swap(1 - core, away))
+    score((1 - core) * 2 + near)
+    go(swap(1 - core, near))
+    merge(away)
+    go(sum_up(y + 4, 0, 0))
+    go(sum_down(y - 4, 1, 0))
+    score(core * 2 + near)
+    merge(near)
+    go(sum_up(y + 3, 1, 1))
+    go(sum_down(y - 3, 0, 1))
 
     ga, gb, gc, gd = quarter(dq[...])
     ha, hb, hc, hd = quarter(ends[pl.ds(0, TRIP), :])
@@ -316,6 +378,8 @@
 
     ret[rel] = gt[rel]
     back(0)
+    neg_step(1, 0)
+    back(1)
     dua = ga * ha + gb * hb + gc * hc + gd * hd
     dub = gb * ha - ga * hb + gc * hd - gd * hc
     duc = gc * ha - ga * hc - gb * hd + gd * hb
@@ -330,62 +394,33 @@
         for g in range(2):
             for w in range(4):
                 at = yy * 16 + g * 8
-                ring[yy, ZX + g * 4 + w] = parts[w][at : at + 8, :]
-
-    for h in (0, 1):
-        swap(core, h).wait_recv()
-
-    @pl.loop(0, NY)
-    def _(k):
-        ring[k, pl.ds(0, ZX)] = gall[core * NY + k] + xrecv[k]
-
-    def chunk(yy, h):
-        return ring.at[lax.rem(yy + 2 * NY, NY), pl.ds(h * CUT, CUT)]
-
-    def take(yy, h, got, n):
-        i = lax.rem(yy + 2 * NY, NY)
-        cols = pl.ds(h * CUT, CUT)
-        ring[i, cols] = ring[i, cols] + got[n, cols]
-
-    def sum_up(yy, h, n):
-        at = 2 * n + h
-        dst = rp.at[n, pl.ds(h * CUT, CUT)]
-        return rcopy(chunk(yy, h), dst, rp_s.at[at], rp_r.at[at], up_dev)
-
-    def sum_down(yy, h, n):
-        at = 2 * n + h
-        dst = rm.at[n, pl.ds(h * CUT, CUT)]
-        return rcopy(chunk(yy, h), dst, rm_s.at[at], rm_r.at[at], down_dev)
-
-    go(sum_up(y + 4, 0, 0))
-    go(sum_down(y - 4, 1, 0))
-    go(sum_up(y + 3, 1, 1))
-    go(sum_down(y - 3, 0, 1))
-
-    for n in (1, 2, 3):
+                rring[yy, g * 4 + w] = parts[w][at : at + 8, :]
+    go(rel_up(0))
+    go(rel_down(0))
+
+    for n in (2, 3):
         for h in (1, 0):
-            if n > 1 or h == 0:
-                sum_up(y + 4 - n, h, n - 1).wait_recv()
-                take(y + 4 - n, h, rp, n - 1)
-                go(sum_up(y + 4 - n, h, n))
-                sum_down(y - 4 + n, 1 - h, n - 1).wait_recv()
-                take(y - 4 + n, 1 - h, rm, n - 1)
-                go(sum_down(y - 4 + n, 1 - h, n))
-                back(2 * n - 1 - h)
+            neg_step(n, h)
+            back(2 * n - 1 - h)
+        rel_step(n - 1)
     for h in (1, 0):
         sum_up(y, h, 3).wait_recv()
         sum_down(y, 1 - h, 3).wait_recv()
     ring[y] = ring[y] + (rp[3] + rm[3])
 
     far = {"dom": (1 - zh) * NY + y}
-    cross = rcopy(ring.at[y, pl.ds(ZX, 8)], relx, rx_s, rx_r, far)
-    go(cross)
+    cross = rcopy(rring.at[y], relx, rx_s, rx_r, far)
 
     @pl.loop(0, ZX - 1)
     def _(k):
         p = zx_peer(k)
         rcopy(ring.at[y, p], zx_recv.at[zi], z_s.at[k], z_r.at[zi], zx_dev(p)).start()
 
+    rel_step(3)
+    rel_up(3).wait_recv()
+    rel_down(3).wait_recv()
+    rring[y] = rring[y] + (rrp[3] + rrm[3])
+    go(cross)
     back(6)
     zx_recv[zi] = ring[y, zi]
 
@@ -403,7 +438,7 @@
 
     t_recv[dom] = tile_out[...]
     cross.wait_recv()
-    rel_full[y] = ring[y, pl.ds(ZX, 8)] + relx[...]
+    rel_full[y] = rring[y] + relx[...]
 
     @pl.loop(1, NY)
     def _(k):
@@ -513,11 +548,14 @@
             pltpu.VMEM((RELS, WIDTH // 4), F32),
             pltpu.VMEM((TRIP, WIDTH), BF16),
             pltpu.VMEM((TRIP, WIDTH), BF16),
+            pltpu.VMEM((NY, 8, *TILE), F32),
+            pltpu.VMEM((4, 8, *TILE), F32),
+            pltpu.VMEM((4, 8, *TILE), F32),
             pltpu.VMEM((2 * NY, ZX, *TILE), F32),
             pltpu.VMEM((NY, ZX, *TILE), F32),
-            pltpu.VMEM((NY, ZX + 8, *TILE), F32),
-            pltpu.VMEM((4, ZX + 8, *TILE), F32),
-            pltpu.VMEM((4, ZX + 8, *TILE), F32),
+            pltpu.VMEM((NY, ZX, *TILE), F32),
+            pltpu.VMEM((4, ZX, *TILE), F32),
+            pltpu.VMEM((4, ZX, *TILE), F32),
             pltpu.VMEM((ZX, *TILE), F32),
             pltpu.VMEM((8, *TILE), F32),
             pltpu.VMEM(TILE, F32),
@@ -532,6 +570,7 @@
             dma((8,)), dma((8,)), dma((8,)), dma((8,)),
             dma((ZX,)), dma((ZX,)), dma, dma,
             dma((N_DOM,)), dma((N_DOM,)), dma((NY,)), dma((NY,)),
+            dma((4,)), dma((4,)), dma((4,)), dma((4,)),
         ],
         compiler_params=pltpu.CompilerParams(
             collective_id=0, has_side_effects=True, vmem_limit_bytes=56 << 20

time: 100 us -> 98.4 us (0.984)
  Pallas kernels: 96.1 us -> 93.9 us
    pallas_call x1, Pallas kernels: 96.1 us -> 93.9 us  [shards(): pl.pallas_call(kernel, out_shape=(rows, rows), in_specs=[anywhere] * 8, o...]
where the time goes in v5:
time: 98.4 us; the launch traced here: 97.4 us
  Pallas kernels  93.9 us (95%)
  other arithmetic  2.22 us (2%)
  between operations  1.32 us (1%)
    pallas_call x1, Pallas kernels, shards(): pl.pallas_call(kernel, out_shape=(rows, rows), in_specs=[anywhere] * 8, o...  93.9 us
    sub x1, other arithmetic, adagrad(): return (values - step_size * gradient / jnp.sqrt(history_new), history_new)  2.22 us

profile of v5, /device:TPU:1, one launch (start us, length us, event | category | flops | bytes accessed | tf_op | source)
XLA Modules:
  0.0 97.4 jit_solution(13991196128897326233)
XLA Ops:
  1.3 0.0 copy-start
  1.3 0.0 copy-start.1
  1.3 93.9 %step.1 = (f32[128,512]{1,0:T(8,128)}, f32[128,512]{1,0:T(8,128)}) custom-call(f32[128,512]{1,0:T(8,128)} %entity_h.1, f32[128,512]{1,0:T(8,128)} %relation_h.1, s32[16,32]{1,0:T(8,128)} %bitcast.8, s32[1,256]{1,0:T(1,128)} %bitcast.9, s32[1,256]{1,0:T(1,128)} %bitcast.10, s32[1,256]{1,0:T(1,128)} %bitcast.11, s32[32,32]{1,0:T(8,128)} %neg_h.1, ...), custom_call_target="tpu_custom_call" | custom-call | tf_op jit(solution)/shard_map/step/pallas_call | solution.py:521
  95.2 0.0 copy-done
  95.2 0.0 copy-done.1
  95.2 2.2 %multiply_subtract_fusion = (f32[128,512]{1,0:T(8,128)}, f32[128,512]{1,0:T(8,128)}, f32[128,512]{1,0:T(8,128)}, f32[128,512]{1,0:T(8,128)}) fusion(f32[128,512]{1,0:T(8,128)S(1)} %copy-done, f32[128,512]{1,0:T(8,128)} %get-tuple-element.7, f32[128,512]{1,0:T(8,128)} %param.13, f32[128,512]{1,0:T(8,128)S(1)} %copy-done.1, f32[128,512]{1,0:T(8,128)} %param.11, ...), kind=kLoop, calls=%fused_computation | loop fusion | flops 655360 | bytes 2621440 | tf_op jit(solution)/shard_map/sub | solution.py:75
Async XLA Ops:
  1.3 93.9 %copy-start = (f32[128,512]{1,0:T(8,128)S(1)}, f32[128,512]{1,0:T(8,128)}, u32[]{:S(2)}) copy-start(f32[128,512]{1,0:T(8,128)} %relation_h.1) | copy-start | bytes 786436
  1.3 93.9 %copy-start.1 = (f32[128,512]{1,0:T(8,128)S(1)}, f32[128,512]{1,0:T(8,128)}, u32[]{:S(2)}) copy-start(f32[128,512]{1,0:T(8,128)} %entity_h.1) | copy-start | bytes 786436

commit v6 on v5

--- a/solution.py
+++ b/solution.py
@@ -81,10 +81,10 @@
     entity, relation, send_t, head_row, tail_row, rels_row, neg_rows, neg_part,
     send_buf, recv, neg_src, s1_recv, nbuf, hot_ends, ends, rot, query, dq, dends,
     rel_hot, unit, scale, q_hi, q_lo, rring, rrp, rrm,
-    gall, xrecv, ring, rp, rm, zx_recv, relx, tile_out, t_recv, rel_full, gt, ret,
+    gall, xrecv, ring, rp, rm, zx_recv, relx, cand, far_recv, t_recv, rel_full, gt, ret,
     in_s, a_s, a_r, b_s, b_r, s1_s, s1_r, s2_s, s2_r, yp_s, yp_r, ym_s, ym_r, sib_s, sib_r, x_s, x_r,
     rp_s, rp_r, rm_s, rm_r, z_s, z_r, rx_s, rx_r, t_s, t_r, ra_s, ra_r,
-    up_s, up_r, dn_s, dn_r,
+    up_s, up_r, dn_s, dn_r, f_s, f_r,
 ):
     loads = [
         pltpu.make_async_copy(h, v, in_s.at[n])
@@ -114,17 +114,17 @@
     def zx_peer(j):
         return lax.rem(zi + fan(j, ZX), ZX)
 
-    def dom_peer(j):
-        other = lax.rem(zh + 1 - lax.div(j, NY), 2)
-        return other * NY + lax.rem(y + fan(lax.rem(j, NY), NY), NY)
+    def y_peer(j):
+        return lax.rem(y + fan(j, NY), NY)
+
+    far = {"dom": (1 - zh) * NY + y}
 
     barrier = pltpu.get_barrier_semaphore()
 
-    @pl.loop(0, N_DOM - 1)
-    def _(k):
-        pl.semaphore_signal(
-            barrier, inc=1, device_id={"dom": dom_peer(k)}, device_id_type=MESH
-        )
+    @pl.loop(0, NY - 1)
+    def _(k):
+        to = {"dom": zh * NY + y_peer(k)}
+        pl.semaphore_signal(barrier, inc=1, device_id=to, device_id_type=MESH)
 
     @pl.loop(1, N_REL)
     def _(k):
@@ -132,7 +132,7 @@
             barrier, inc=1, device_id={"rel": lax.rem(rel + k, N_REL)}, device_id_type=MESH
         )
 
-    @pl.loop(1, 16)
+    @pl.loop(0, 16)
     def _(k):
         p = (1 - zh) * 16 + lax.rem(zx_low + k, 16)
         pl.semaphore_signal(barrier, inc=1, device_id=zx_dev(p), device_id_type=MESH)
@@ -144,20 +144,33 @@
     own = mm(neg_hot, ent[0], TN) + mm(neg_hot, ent[1], TN)
     for g in range(4):
         for w in range(4):
-            neg_src[g * 4 + w] = own[g * 8 : g * 8 + 8, w * 128 : w * 128 + 128]
+            neg_src[(g % 2) * 4 + w, g // 2] = own[g * 8 : g * 8 + 8, w * 128 : w * 128 + 128]
     send_hot = hot(ENT, slot_row(send_t))
     rows = mm(send_hot, ent[0], TN) + mm(send_hot, ent[1], TN)
     send_buf[...] = rows.reshape(N_REL, SLOTS, WIDTH)
     for c in loads[4:]:
         c.wait()
-    is_root = lax.broadcasted_iota(jnp.int32, (N_DOM, 1, 1), 0) == neg_part[...].reshape(1, 1, 1)
-
-    pl.semaphore_wait(barrier, (N_DOM - 1) + (N_REL - 1) + 15)
-
-    @pl.loop(0, N_DOM - 1)
-    def _(k):
-        p = dom_peer(k)
-        rcopy(neg_src.at[p], s1_recv.at[dom], s1_s.at[k], s1_r.at[dom], {"dom": p}).start()
+    root_y = lax.rem(neg_part[...], NY).reshape(1, 1, 1, 1)
+    is_root = lax.broadcasted_iota(jnp.int32, (NY, 1, 1, 1), 0) == root_y
+
+    pl.semaphore_wait(barrier, (NY - 1) + (N_REL - 1) + 16)
+
+    def scatter(k, slot):
+        p = y_peer(k)
+        at = y if slot is None else p
+        return rcopy(
+            neg_src.at[p], s1_recv.at[at], s1_s.at[k], s1_r.at[at], {"dom": zh * NY + p}
+        )
+
+    @pl.loop(0, NY - 1)
+    def _(k):
+        scatter(k, None).start()
+
+    sent = []
+
+    def go(c):
+        c.start()
+        sent.append(c)
 
     def peer(k):
         pz = lax.rem(lax.div(rel, 8) + lax.rem(k, 4), 4)
@@ -179,16 +192,20 @@
 
     ahead(0)
 
-    s1_recv[dom] = neg_src[dom]
+    s1_recv[y] = neg_src[y]
     recv[rel] = send_buf[rel]
 
-    @pl.loop(0, N_DOM - 1)
-    def _(k):
-        p = dom_peer(k)
-        rcopy(neg_src.at[p], s1_recv.at[p], s1_s.at[k], s1_r.at[p], {"dom": p}).wait_recv()
-
+    @pl.loop(0, NY - 1)
+    def _(k):
+        scatter(k, 0).wait_recv()
+
+    cand[...] = jnp.sum(jnp.where(is_root, s1_recv[...], 0.0), axis=0)
+    over = rcopy(cand.at[1 - zh], far_recv, f_s.at[0], f_r.at[0], far)
+    go(over)
+    over.wait_recv()
     mine = core * NY + y
-    nbuf[mine, zi] = jnp.sum(jnp.where(is_root, s1_recv[...], 0.0), axis=0)
+    here = lax.div(neg_part[...], NY) == zh
+    nbuf[mine, zi] = jnp.where(here, cand[zh], far_recv[...])
 
     @pl.loop(0, ZX - 1)
     def _(k):
@@ -219,12 +236,6 @@
         ref = part(core_of, y + off, h)
         at = 2 * (off + 4) + h
         return rcopy(ref, ref, sib_s.at[at], sib_r.at[at], sib_dev)
-
-    sent = []
-
-    def go(c):
-        c.start()
-        sent.append(c)
 
     for h in (0, 1):
         go(pass_up(y, h, 0))
@@ -408,7 +419,6 @@
         sum_down(y, 1 - h, 3).wait_recv()
     ring[y] = ring[y] + (rp[3] + rm[3])
 
-    far = {"dom": (1 - zh) * NY + y}
     cross = rcopy(rring.at[y], relx, rx_s, rx_r, far)
 
     @pl.loop(0, ZX - 1)
@@ -429,14 +439,8 @@
         p = zx_peer(k)
         rcopy(ring.at[y, p], zx_recv.at[p], z_s.at[k], z_r.at[p], zx_dev(p)).wait_recv()
 
-    tile_out[...] = jnp.sum(zx_recv[...], axis=0)
-
-    @pl.loop(0, N_DOM - 1)
-    def _(k):
-        p = dom_peer(k)
-        rcopy(tile_out, t_recv.at[dom], t_s.at[k], t_r.at[dom], {"dom": p}).start()
-
-    t_recv[dom] = tile_out[...]
+    t_recv[y, zh] = jnp.sum(zx_recv[...], axis=0)
+    go(rcopy(t_recv.at[y, zh], t_recv.at[y, zh], f_s.at[1], f_r.at[1], far))
     cross.wait_recv()
     rel_full[y] = rring[y] + relx[...]
 
@@ -445,6 +449,20 @@
         to = {"dom": zh * NY + lax.rem(y + k, NY)}
         rcopy(rel_full.at[y], rel_full.at[y], ra_s.at[k], ra_r.at[y], to).start()
 
+    there = t_recv.at[y, 1 - zh]
+    rcopy(there, there, f_s.at[1], f_r.at[1], far).wait_recv()
+
+    def gather(k, slot):
+        p = y_peer(k)
+        at = y if slot is None else p
+        return rcopy(
+            t_recv.at[at], t_recv.at[at], t_s.at[k], t_r.at[at], {"dom": zh * NY + p}
+        )
+
+    @pl.loop(0, NY - 1)
+    def _(k):
+        gather(k, None).start()
+
     @pl.loop(1, N_REL)
     def _(k):
         p = lax.rem(rel + k, N_REL)
@@ -453,14 +471,13 @@
     send_hot = hot(ENT, slot_row(send_t))
     grad = select(send_hot, ret[...].reshape(N_REL * SLOTS, WIDTH), NN)
 
-    @pl.loop(0, N_DOM - 1)
-    def _(k):
-        p = dom_peer(k)
-        rcopy(tile_out, t_recv.at[p], t_s.at[k], t_r.at[p], {"dom": p}).wait_recv()
+    @pl.loop(0, NY - 1)
+    def _(k):
+        gather(k, 0).wait_recv()
 
     total = jnp.concatenate(
         [
-            jnp.concatenate([t_recv[g * 4 + w] for w in range(4)], axis=1)
+            jnp.concatenate([t_recv[(g % 2) * 4 + w, g // 2] for w in range(4)], axis=1)
             for g in range(4)
         ],
         axis=0,
@@ -484,11 +501,10 @@
     for c in sent:
         c.wait_send()
 
-    @pl.loop(0, N_DOM - 1)
-    def _(k):
-        p = dom_peer(k)
-        rcopy(neg_src.at[p], s1_recv.at[dom], s1_s.at[k], s1_r.at[dom], {"dom": p}).wait_send()
-        rcopy(tile_out, t_recv.at[dom], t_s.at[k], t_r.at[dom], {"dom": p}).wait_send()
+    @pl.loop(0, NY - 1)
+    def _(k):
+        scatter(k, None).wait_send()
+        gather(k, None).wait_send()
 
     @pl.loop(1, N_REL)
     def _(k):
@@ -534,8 +550,8 @@
             pltpu.VMEM((1, 1), jnp.int32),
             pltpu.VMEM((N_REL, SLOTS, WIDTH), F32),
             pltpu.VMEM((N_REL, SLOTS, WIDTH), F32),
-            pltpu.VMEM((N_DOM, *TILE), F32),
-            pltpu.VMEM((N_DOM, *TILE), F32),
+            pltpu.VMEM((NY, 2, *TILE), F32),
+            pltpu.VMEM((NY, 2, *TILE), F32),
             pltpu.VMEM((2 * NY, ZX, *TILE), F32),
             pltpu.VMEM((N_REL * SLOTS, 2 * TRIP), BF16),
             pltpu.VMEM((2 * TRIP, WIDTH), F32),
@@ -558,19 +574,20 @@
             pltpu.VMEM((4, ZX, *TILE), F32),
             pltpu.VMEM((ZX, *TILE), F32),
             pltpu.VMEM((8, *TILE), F32),
+            pltpu.VMEM((2, *TILE), F32),
             pltpu.VMEM(TILE, F32),
-            pltpu.VMEM((N_DOM, *TILE), F32),
+            pltpu.VMEM((NY, 2, *TILE), F32),
             pltpu.VMEM((NY, 8, *TILE), F32),
             pltpu.VMEM((N_REL, SLOTS, WIDTH), F32),
             pltpu.VMEM((N_REL, SLOTS, WIDTH), F32),
             dma((8,)), dma((N_REL,)), dma((N_REL,)), dma((N_REL,)), dma((N_REL,)),
-            dma((N_DOM,)), dma((N_DOM,)), dma((ZX,)), dma((ZX,)),
+            dma((NY,)), dma((NY,)), dma((ZX,)), dma((ZX,)),
             dma((8,)), dma((8,)), dma((8,)), dma((8,)),
             dma((16,)), dma((16,)), dma((2,)), dma((2,)),
             dma((8,)), dma((8,)), dma((8,)), dma((8,)),
             dma((ZX,)), dma((ZX,)), dma, dma,
-            dma((N_DOM,)), dma((N_DOM,)), dma((NY,)), dma((NY,)),
-            dma((4,)), dma((4,)), dma((4,)), dma((4,)),
+            dma((NY,)), dma((NY,)), dma((NY,)), dma((NY,)),
+            dma((4,)), dma((4,)), dma((4,)), dma((4,)), dma((2,)), dma((2,)),
         ],
         compiler_params=pltpu.CompilerParams(
             collective_id=0, has_side_effects=True, vmem_limit_bytes=56 << 20

time: 98.4 us -> 101 us (1.026)
  the two profiles are of different devices: /device:TPU:1 before, /device:TPU:8 now
where the time goes in v6:
time: 101 us; the launch traced here: 100 us
  Pallas kernels  96.8 us (96%)
  other arithmetic  2.22 us (2%)
  between operations  1.32 us (1%)
    pallas_call x1, Pallas kernels, shards(): pl.pallas_call(kernel, out_shape=(rows, rows), in_specs=[anywhere] * 8, o...  96.8 us
    sub x1, other arithmetic, adagrad(): return (values - step_size * gradient / jnp.sqrt(history_new), history_new)  2.22 us

profile of v6, /device:TPU:8, one launch (start us, length us, event | category | flops | bytes accessed | tf_op | source)
XLA Modules:
  0.0 100.4 jit_solution(1113442287567128822)
XLA Ops:
  1.3 0.0 copy-start
  1.3 0.0 copy-start.1
  1.3 96.8 %step.1 = (f32[128,512]{1,0:T(8,128)}, f32[128,512]{1,0:T(8,128)}) custom-call(f32[128,512]{1,0:T(8,128)} %entity_h.1, f32[128,512]{1,0:T(8,128)} %relation_h.1, s32[16,32]{1,0:T(8,128)} %bitcast.8, s32[1,256]{1,0:T(1,128)} %bitcast.9, s32[1,256]{1,0:T(1,128)} %bitcast.10, s32[1,256]{1,0:T(1,128)} %bitcast.11, s32[32,32]{1,0:T(8,128)} %neg_h.1, ...), custom_call_target="tpu_custom_call" | custom-call | tf_op jit(solution)/shard_map/step/pallas_call | solution.py:537
  98.1 0.0 copy-done
  98.1 0.0 copy-done.1
  98.1 2.2 %multiply_subtract_fusion = (f32[128,512]{1,0:T(8,128)}, f32[128,512]{1,0:T(8,128)}, f32[128,512]{1,0:T(8,128)}, f32[128,512]{1,0:T(8,128)}) fusion(f32[128,512]{1,0:T(8,128)S(1)} %copy-done, f32[128,512]{1,0:T(8,128)} %get-tuple-element.7, f32[128,512]{1,0:T(8,128)} %param.13, f32[128,512]{1,0:T(8,128)S(1)} %copy-done.1, f32[128,512]{1,0:T(8,128)} %param.11, ...), kind=kLoop, calls=%fused_computation | loop fusion | flops 655360 | bytes 2621440 | tf_op jit(solution)/shard_map/sub | solution.py:75
Async XLA Ops:
  1.3 96.8 %copy-start = (f32[128,512]{1,0:T(8,128)S(1)}, f32[128,512]{1,0:T(8,128)}, u32[]{:S(2)}) copy-start(f32[128,512]{1,0:T(8,128)} %relation_h.1) | copy-start | bytes 786436
  1.3 96.8 %copy-start.1 = (f32[128,512]{1,0:T(8,128)S(1)}, f32[128,512]{1,0:T(8,128)}, u32[]{:S(2)}) copy-start(f32[128,512]{1,0:T(8,128)} %entity_h.1) | copy-start | bytes 786436

commit v7 on v5

--- a/solution.py
+++ b/solution.py
@@ -16,7 +16,7 @@
 TILE = (8, 128)
 NEGS = NEG * N_REL
 AHEAD = (8, 12, 15, 18, 21, 24, 27, 32)
-BACK = (9, 12, 14, 16, 18, 20, 32)
+BACK = (12, 15, 18, 20, 22, 24, 32)
 HALF = ZX // 2
 
 NN = (((1,), (0,)), ((), ()))

time: 98.4 us -> 103 us (1.047)
  Pallas kernels: 93.9 us -> 98.5 us
    pallas_call x1, Pallas kernels: 93.9 us -> 98.5 us  [shards(): pl.pallas_call(kernel, out_shape=(rows, rows), in_specs=[anywhere] * 8, o...]
where the time goes in v7:
time: 103 us; the launch traced here: 102 us
  Pallas kernels  98.5 us (96%)
  other arithmetic  2.22 us (2%)
  between operations  1.32 us (1%)
    pallas_call x1, Pallas kernels, shards(): pl.pallas_call(kernel, out_shape=(rows, rows), in_specs=[anywhere] * 8, o...  98.5 us
    sub x1, other arithmetic, adagrad(): return (values - step_size * gradient / jnp.sqrt(history_new), history_new)  2.22 us

profile of v7, /device:TPU:1, one launch (start us, length us, event | category | flops | bytes accessed | tf_op | source)
XLA Modules:
  0.0 102.0 jit_solution(4117948898680301192)
XLA Ops:
  1.3 0.0 copy-start
  1.3 0.0 copy-start.1
  1.3 98.5 %step.1 = (f32[128,512]{1,0:T(8,128)}, f32[128,512]{1,0:T(8,128)}) custom-call(f32[128,512]{1,0:T(8,128)} %entity_h.1, f32[128,512]{1,0:T(8,128)} %relation_h.1, s32[16,32]{1,0:T(8,128)} %bitcast.8, s32[1,256]{1,0:T(1,128)} %bitcast.9, s32[1,256]{1,0:T(1,128)} %bitcast.10, s32[1,256]{1,0:T(1,128)} %bitcast.11, s32[32,32]{1,0:T(8,128)} %neg_h.1, ...), custom_call_target="tpu_custom_call" | custom-call | tf_op jit(solution)/shard_map/step/pallas_call | solution.py:521
  99.8 0.0 copy-done
  99.8 0.0 copy-done.1
  99.8 2.2 %multiply_subtract_fusion = (f32[128,512]{1,0:T(8,128)}, f32[128,512]{1,0:T(8,128)}, f32[128,512]{1,0:T(8,128)}, f32[128,512]{1,0:T(8,128)}) fusion(f32[128,512]{1,0:T(8,128)S(1)} %copy-done, f32[128,512]{1,0:T(8,128)} %get-tuple-element.7, f32[128,512]{1,0:T(8,128)} %param.13, f32[128,512]{1,0:T(8,128)S(1)} %copy-done.1, f32[128,512]{1,0:T(8,128)} %param.11, ...), kind=kLoop, calls=%fused_computation | loop fusion | flops 655360 | bytes 2621440 | tf_op jit(solution)/shard_map/sub | solution.py:75
Async XLA Ops:
  1.3 98.5 %copy-start = (f32[128,512]{1,0:T(8,128)S(1)}, f32[128,512]{1,0:T(8,128)}, u32[]{:S(2)}) copy-start(f32[128,512]{1,0:T(8,128)} %relation_h.1) | copy-start | bytes 786436
  1.3 98.5 %copy-start.1 = (f32[128,512]{1,0:T(8,128)S(1)}, f32[128,512]{1,0:T(8,128)}, u32[]{:S(2)}) copy-start(f32[128,512]{1,0:T(8,128)} %entity_h.1) | copy-start | bytes 786436
